TPU v7x, 128 devices: a whole 4x4x4 slice. The times are simulated.
128 devices in a mesh: kv: 2 (over core), seq: 64 (over z, y, x), dp: 1.
Axes of the slice: x: 4, y: 4, z: 4, core: 2. Of those that a mesh axis runs over, the one named last changes fastest.
Arguments:
- token_input_state: bfloat16 [4, 8192], P('dp'), may hold values from -6 to 6
- query_matrix: bfloat16 [8192, 2048], P('seq', 'kv'), may hold values from -0.0625 to 0.0625
- key_value_weight: bfloat16 [8192, 512], P('seq', 'kv'), may hold values from -0.5 to 0.5
- output_weight: bfloat16 [2048, 8192], P('kv', 'seq'), may hold values from -0.125 to 0.125
- key_cache_rows: bfloat16 [4, 2, 131072, 128], P('dp', 'kv', 'seq'), may hold values from -6000 to 6000, as said below
- value_cache_rows: bfloat16 [4, 2, 131072, 128], P('dp', 'kv', 'seq'), may hold values from -24 to 24
- live_lengths: int32 [4, 64], P('dp'), may hold values from 2 to 2048, as said below
- owner_shard: int32 [4], P('dp'), may hold values from 0 to 63
Outputs:
- layer_out: bfloat16 [4, 8192], P('dp', 'seq')
Inputs may be any that keep to these rules, and one draw needn't show every extreme that they name: `live_lengths`: every block holds 2 to 2048 live slots; the owner's block of a sequence holds fewer than 2048; in every sequence some other block holds exactly 2048. `key_cache_rows`: bounded as stated.
All inputs are finite; a program needn't handle non-finite values.
Results may differ from a plain program's by a relative error of at most 0.015.
The roundings to bfloat16 on the way count: a program that leaves them out, or rounds other values in their place, can miss the bound.
Values may be sent and summed in bfloat16 or wider, within the bound.
No kernel may reach another device: no remote copies, remote signals or barrier semaphores. Data moves between devices by JAX's collectives and lax.ppermute only.
A program may use at most 64 MiB of HBM per device.

v0:
```python
import math

import jax
import jax.numpy as jnp
from jax import lax
from jax.sharding import Mesh
from jax.sharding import PartitionSpec as P

HEAD_SIZE = 128
QUERY_GROUP = 8
SEQ = ("seq_0", "seq_1", "seq_2")


rope_theta = 500000.0


def copy_for_each(array, axis):
    count = lax.axis_size(axis)
    return lax.all_to_all(
        jnp.broadcast_to(array[None], (count, *array.shape)), axis, 0, 0, tiled=True
    )


def of_everyone(array, axis):
    return copy_for_each(array, axis).sum(axis=0)


def packed_total(arrays, axis):
    vector, at, outs = (jnp.concatenate([a.reshape(-1) for a in arrays]), 0, [])
    running = of_everyone(vector, axis)
    for a in arrays:
        outs.append(running[at : at + a.size].reshape(a.shape))
        at += a.size
    return tuple(outs)


def collected_together(array, axis):
    leaves = jax.tree.leaves(array)
    order = sorted(range(len(leaves)), key=lambda k: -leaves[k].size)
    width = (1, *leaves[order[0]].shape)[-1]
    lines = [
        jnp.pad(leaves[k].reshape(-1), (0, -leaves[k].size % width)).reshape(-1, width)
        for k in order
    ]
    both, at, found = (lax.all_gather(jnp.concatenate(lines), axis), 0, {})
    for k, line in zip(order, lines):
        section = both[:, at : at + len(line)].reshape(len(both), -1)
        found[k] = section[:, : leaves[k].size].reshape(-1, *leaves[k].shape)
        at += len(line)
    numbers = iter(range(len(leaves)))
    return jax.tree.map(lambda _: found[next(numbers)], array)


def merged_by_axis(array, axes, combine):
    for axis in axes:
        pieces = collected_together(array, axis)
        array = jax.tree.map(lambda part: part[0], pieces)
        for k in range(1, lax.axis_size(axis)):
            array = combine(array, jax.tree.map(lambda part: part[k], pieces))
    return array


def over_pieces(array, axis):
    tiles = lax.all_gather(array, axis)
    return tiles.sum(axis=0)


def frequencies():
    exponent = jnp.arange(0, HEAD_SIZE, 2).astype(jnp.float32) / HEAD_SIZE
    return jnp.power(rope_theta, -exponent)


def rotate(vectors, angles):
    half_size = vectors.shape[-1] // 2
    first_half = vectors[..., :half_size]
    second_half = vectors[..., half_size:]
    cosine_table = jnp.cos(angles)
    sine_table = jnp.sin(angles)
    return jnp.concatenate(
        [
            first_half * cosine_table - second_half * sine_table,
            second_half * cosine_table + first_half * sine_table,
        ],
        -1,
    )


def combine_parts(earlier, later):
    shard_top = jnp.maximum(earlier[0], later[0])
    early_factor = jnp.exp(earlier[0] - shard_top)
    late_factor = jnp.exp(later[0] - shard_top)
    totals = earlier[1] * early_factor + later[1] * late_factor
    accum = earlier[2] * early_factor[..., None] + later[2] * late_factor[..., None]
    return (shard_top, totals, accum)


def local(
    token_input_state,
    query_matrix,
    key_value_weight,
    output_weight,
    key_cache_rows,
    value_cache_rows,
    live_lengths,
    owner_shard,
):
    batch_rows = token_input_state.shape[0]
    kv_local = key_cache_rows.shape[1]
    slot_count = key_cache_rows.shape[2]
    row_count = query_matrix.shape[0]
    shard_index = lax.axis_index(SEQ)
    shard_total = lax.axis_size(SEQ)
    local_cols = lax.dynamic_slice_in_dim(token_input_state, shard_index * row_count, row_count, 1)
    query_part = jnp.dot(local_cols, query_matrix, preferred_element_type=jnp.float32)
    keyval_part = jnp.dot(local_cols, key_value_weight, preferred_element_type=jnp.float32)
    query_flat, keyval_flat = packed_total((query_part, keyval_part), SEQ)
    query_rows = query_flat.reshape(batch_rows, kv_local, QUERY_GROUP, HEAD_SIZE)
    key_value_rows = keyval_flat.reshape(batch_rows, kv_local, 2, HEAD_SIZE)
    columns = jnp.arange(shard_total)[None, :]
    lookup = jnp.sum(jnp.where(columns == owner_shard[:, None], live_lengths, 0), 1)
    own_length = jnp.sum(jnp.where(columns == shard_index, live_lengths, 0), 1)
    position = owner_shard * slot_count + lookup
    angles = position.astype(jnp.float32)[:, None] * frequencies()[None, :]
    query_rot = rotate(query_rows, angles[:, None, None, :]).astype(jnp.bfloat16)
    key_new = rotate(key_value_rows[:, :, 0], angles[:, None, :]).astype(jnp.bfloat16)
    value_new = key_value_rows[:, :, 1].astype(jnp.bfloat16)
    scaling = 1.0 / math.sqrt(HEAD_SIZE)
    new_score = (
        jnp.sum(query_rot.astype(jnp.float32) * key_new.astype(jnp.float32)[:, :, None, :], -1)
        * scaling
    )
    is_owner = (owner_shard == shard_index)[:, None, None]
    start_top = jnp.where(is_owner, new_score, -jnp.inf)
    scores = (
        jnp.einsum("bhgd,bhld->bhgl", query_rot, key_cache_rows, preferred_element_type=jnp.float32)
        * scaling
    )
    live_mask = jnp.arange(slot_count)[None, :] < own_length[:, None]
    scores = jnp.where(live_mask[:, None, None, :], scores, -jnp.inf)
    shard_top = jnp.maximum(jnp.max(scores, -1), start_top)
    prob_block = jnp.exp(scores - shard_top[..., None]).astype(jnp.bfloat16)
    totals = jnp.sum(prob_block, -1, dtype=jnp.float32)
    accum = jnp.einsum(
        "bhgl,bhld->bhgd", prob_block, value_cache_rows, preferred_element_type=jnp.float32
    )
    new_prob = jnp.where(is_owner, jnp.exp(new_score - shard_top), 0.0).astype(jnp.bfloat16)
    totals = totals + new_prob.astype(jnp.float32)
    accum = (
        accum
        + new_prob.astype(jnp.float32)[..., None] * value_new.astype(jnp.float32)[:, :, None, :]
    )
    overall, totals, accum = merged_by_axis((shard_top, totals, accum), SEQ, combine_parts)
    attended = (
        (accum / totals[..., None])
        .astype(jnp.bfloat16)
        .reshape(batch_rows, kv_local * QUERY_GROUP * HEAD_SIZE)
    )
    partial_value = jnp.dot(attended, output_weight, preferred_element_type=jnp.float32)
    return over_pieces(partial_value, "kv").astype(jnp.bfloat16)


def solution(mesh):
    finer = Mesh(
        mesh.devices.reshape(mesh.shape["kv"], 4, 4, 4, mesh.shape["dp"]),
        ("kv", "seq_0", "seq_1", "seq_2", "dp"),
    )
    return jax.shard_map(
        local,
        mesh=finer,
        in_specs=(
            P("dp", None),
            P(SEQ, "kv"),
            P(SEQ, "kv"),
            P("kv", SEQ),
            P("dp", "kv", SEQ, None),
            P("dp", "kv", SEQ, None),
            P("dp", None),
            P("dp"),
        ),
        out_specs=P("dp", SEQ),
        check_vma=False,
    )
```

profile of v0, /device:TPU:1, one launch (start us, length us, event | category | flops | bytes accessed | tf_op | source)
XLA Modules:
  0.0 82.8 jit_solution(18355006144514998695)
XLA Ops:
  0.0 0.0 copy-start
  0.0 1.3 %convolution_bitcast_fusion = f32[1,8,4,128]{3,2,1,0:T(4,128)S(1)} fusion(bf16[128,1024]{1,0:T(8,128)(2,1)} %param.9, bf16[4,8192]{1,0:T(4,128)(2,1)} %param.8, s32[]{:T(128)S(6)} %select_n.49), kind=kOutput, calls=%fused_computation.7 | convolution fusion | flops 1048576 | bytes 279556 | tf_op jit(solution)/shard_map/dot_general | solution.py:114
  1.3 1.0 %convolution_bitcast_fusion.1 = f32[1,2,4,128]{3,2,1,0:T(4,128)S(1)} fusion(bf16[128,256]{1,0:T(8,128)(2,1)} %param.10, bf16[4,8192]{1,0:T(4,128)(2,1)} %param.8, s32[]{:T(128)S(6)} %select_n.49), kind=kOutput, calls=%fused_computation.8 | convolution fusion | flops 262144 | bytes 70660 | tf_op jit(solution)/shard_map/dot_general | solution.py:115
  2.3 1.7 %broadcast_in_dim.57 = f32[64,1,5120]{2,1,0:T(1,128)} broadcast(f32[5120]{0:T(1024)S(1)} %pad_maximum_fusion), dimensions={2} | broadcast | bytes 1331200 | tf_op jit(solution)/shard_map/broadcast_in_dim | solution.py:20
  4.0 12.0 %all-to-all-start = ((f32[64,1,5120]{2,1,0:T(1,128)}), f32[64,1,5120]{2,1,0:T(1,128)S(1)}, u32[]{:S(2)}, u32[]{:S(2)}) async-start(f32[64,1,5120]{2,1,0:T(1,128)} %broadcast_in_dim.57), calls=%async_computation | async-start | bytes 2621440 | tf_op jit(solution)/shard_map/all_to_all | solution.py:19
  16.0 0.0 copy-done.3
  16.0 0.1 broadcast_in_dim.62
  16.1 0.1 broadcast_in_dim.100
  16.2 0.0 copy-done.2
  16.2 0.2 select_reduce_fusion
  16.4 0.1 multiply_cosine_fusion.1
  16.5 0.1 iota_compare_fusion
  16.6 19.8 %all-to-all-done = f32[64,1,5120]{2,1,0:T(1,128)S(1)} async-done(((f32[64,1,5120]{2,1,0:T(1,128)}), f32[64,1,5120]{2,1,0:T(1,128)S(1)}, u32[]{:S(2)}, u32[]{:S(2)}) %all-to-all-start) | async-done | bytes 1310752 | tf_op jit(solution)/shard_map/all_to_all | solution.py:19
  36.5 0.8 reduce_sum.57
  37.3 0.1 fusion.49
  37.4 0.1 maximum_convert_fusion
  37.5 0.1 subtract_convert_fusion
  37.5 0.2 multiply_reduce_fusion
  37.7 0.8 fusion.87
  38.5 0.1 reduce_max.12
  38.6 0.1 fusion.47
  38.6 0.2 convert_reduce_fusion
  38.9 0.1 reduce_sum.61
  38.9 0.1 mul.533
  39.1 2.0 %fusion.7 = f32[32,128]{1,0:T(8,128)S(1)} fusion(bf16[4,1,2048,128]{3,2,1,0:T(8,128)(2,1)} %param.13, f32[4,8,2048]{2,1,0:T(8,128)S(1)} %get-tuple-element.60, f32[4,8]{1,0:T(4,128)S(1)} %get-tuple-element.51, f32[4,128]{1,0:T(4,128)S(1)} %bitcast.328, f32[4,8]{1,0:T(4,128)S(1)} %get-tuple-element.50), kind=kOutput, calls=%fused_computation.6 | convolution fusion | flops 16916480 | bytes 2377984 | tf_op jit(solution)/shard_map/bhgl,bhld->bhgd/dot_general | solution.py:143
  41.1 9.0 %all-gather.4 = f32[4,34,128]{2,1,0:T(8,128)S(1)} all-gather(f32[1,34,128]{2,1,0:T(8,128)S(1)} %maximum_bitcast_fusion), channel_id=2, replica_groups=mesh['kv'=2,'seq_0'=4,'seq_1'=4,'seq_2'=4,'dp'=1] {'seq_0'}, dimensions={0}, use_global_device_ids=true | all-gather | bytes 87040 | tf_op jit(solution)/shard_map/all_gather | solution.py:45
  50.2 0.1 fusion.23
  50.3 9.2 %all-gather.5 = f32[4,34,128]{2,1,0:T(8,128)S(1)} all-gather(f32[1,34,128]{2,1,0:T(8,128)S(1)} %maximum_bitcast_fusion.1), channel_id=3, replica_groups=mesh['kv'=2,'seq_0'=4,'seq_1'=4,'seq_2'=4,'dp'=1] {'seq_1'}, dimensions={0}, use_global_device_ids=true | all-gather | bytes 87040 | tf_op jit(solution)/shard_map/all_gather | solution.py:45
  59.6 0.1 fusion.14
  59.7 9.0 %all-gather.6 = f32[4,34,128]{2,1,0:T(8,128)S(1)} all-gather(f32[1,34,128]{2,1,0:T(8,128)S(1)} %maximum_bitcast_fusion.2), channel_id=4, replica_groups=mesh['kv'=2,'seq_0'=4,'seq_1'=4,'seq_2'=4,'dp'=1] {'seq_2'}, dimensions={0}, use_global_device_ids=true | all-gather | bytes 87040 | tf_op jit(solution)/shard_map/all_gather | solution.py:45
  68.8 0.1 squeeze.138
  68.9 0.1 squeeze.139
  68.9 0.1 squeeze.141
  69.0 0.1 squeeze.143
  69.1 0.1 squeeze.145
  69.2 0.1 squeeze.146
  69.3 0.1 squeeze.147
  69.4 0.1 squeeze.148
  69.5 0.1 broadcast_bitcast_fusion
  69.5 0.1 broadcast_bitcast_fusion.1
  69.6 0.1 broadcast_bitcast_fusion.2
  69.7 0.1 broadcast_bitcast_fusion.3
  69.8 0.1 broadcast_bitcast_fusion.4
  69.8 0.1 broadcast_bitcast_fusion.5
  69.9 0.1 broadcast_bitcast_fusion.6
  70.0 0.2 convolution_bitcast_fusion.2
  70.1 12.1 %all-gather.7 = f32[2,4,128]{2,1,0:T(4,128)S(1)} all-gather(f32[1,4,128]{2,1,0:T(4,128)S(1)} %convolution_bitcast_fusion.2), channel_id=5, replica_groups=mesh['kv'=2,'seq_0'=4,'seq_1'=4,'seq_2'=4,'dp'=1] {'kv'}, dimensions={0}, use_global_device_ids=true | all-gather | bytes 6144 | tf_op jit(solution)/shard_map/all_gather | solution.py:64
  82.2 0.6 reduce_sum.62
  (38 shorter events, 0.3 us)
Async XLA Ops:
  0.0 37.7 %copy-start = (bf16[4,1,2048,128]{3,2,1,0:T(8,128)(2,1)S(1)}, bf16[4,1,2048,128]{3,2,1,0:T(8,128)(2,1)}, u32[]{:S(2)}) copy-start(bf16[4,1,2048,128]{3,2,1,0:T(8,128)(2,1)} %param.12) | copy-start | bytes 6291460
  1.3 14.7 %copy-start.3 = (s32[4]{0:T(128)S(1)}, s32[4]{0:T(128)}, u32[]{:S(2)}) copy-start(s32[4]{0:T(128)} %param.15) | copy-start | bytes 52
  1.3 14.9 %copy-start.2 = (s32[4,64]{1,0:T(4,128)S(1)}, s32[4,64]{1,0:T(4,128)}, u32[]{:S(2)}) copy-start(s32[4,64]{1,0:T(4,128)} %param.14) | copy-start | bytes 3076
  4.0 32.4 %all-to-all-start = ((f32[64,1,5120]{2,1,0:T(1,128)}), f32[64,1,5120]{2,1,0:T(1,128)S(1)}, u32[]{:S(2)}, u32[]{:S(2)}) async-start(f32[64,1,5120]{2,1,0:T(1,128)} %broadcast_in_dim.57), calls=%async_computation | async-start | bytes 2621440 | tf_op jit(solution)/shard_map/all_to_all | solution.py:19
  38.5 31.5 %copy-start.1 = (bf16[1024,128]{1,0:T(8,128)(2,1)S(1)}, bf16[1024,128]{1,0:T(8,128)(2,1)}, u32[]{:S(2)}) copy-start(bf16[1024,128]{1,0:T(8,128)(2,1)} %param.11) | copy-start | bytes 786436
where the time goes:
time: 83.1 us; the launch traced here: 82.8 us
  blocking collectives  39.3 us (47%)
  waiting for transfers between devices  19.8 us (24%)
  starting transfers between devices  12 us (14%)
  matrix products  5.24 us (6%)
  local copies, waits for them, and re-layouts  3.45 us (4%)
  other arithmetic  2.77 us (3%)
    all_gather x3, blocking collectives, collected_together(): both, at, found = (lax.all_gather(jnp.concatenate(lines), axis), 0, {})  27.2 us
    all_to_all x1, waiting for transfers between devices, copy_for_each(): lax.all_to_all(jnp.broadcast_to(array[None], (count, *array.shape)), axis...  19.8 us
    all_gather x1, blocking collectives, over_pieces(): tiles = lax.all_gather(array, axis)  12.1 us
    all_to_all x1, starting transfers between devices, copy_for_each(): lax.all_to_all(jnp.broadcast_to(array[None], (count, *array.shape)), axis...  12 us
    dot_general x1, matrix products, local(): jnp.einsum('bhgl,bhld->bhgd', prob_block, value_cache_rows, preferred_ele...  2.03 us
    broadcast_in_dim x1, local copies, waits for them, and re-layouts, copy_for_each(): jnp.broadcast_to(array[None], (count, *array.shape))  1.75 us
  transfers between devices with their start and end apart: 1, of which 1 were waited for; matrix products, arithmetic and copies ran while one was open for 1% of the time, Pallas kernels for 0%

commit v1 on v0

--- a/solution.py
+++ b/solution.py
@@ -14,55 +14,25 @@
 rope_theta = 500000.0
 
 
-def copy_for_each(array, axis):
-    count = lax.axis_size(axis)
-    return lax.all_to_all(
-        jnp.broadcast_to(array[None], (count, *array.shape)), axis, 0, 0, tiled=True
-    )
+def exchanges(array, axis):
+    beside = lax.ppermute(array, axis, ((0, 1), (1, 0), (2, 3), (3, 2)))
+    around = lax.ppermute(array, axis, ((0, 3), (3, 0), (1, 2), (2, 1)))
+    across = lax.ppermute(array, axis, ((0, 2), (2, 0), (1, 3), (3, 1)))
+    return (array + beside) + (around + across)
 
 
-def of_everyone(array, axis):
-    return copy_for_each(array, axis).sum(axis=0)
+def copies_from(array, axes):
+    count = lax.axis_size(axes)
+    return lax.all_to_all(jnp.broadcast_to(array[None], (count, *array.shape)), axes, 0, 0, tiled=True)
 
 
-def packed_total(arrays, axis):
-    vector, at, outs = (jnp.concatenate([a.reshape(-1) for a in arrays]), 0, [])
-    running = of_everyone(vector, axis)
-    for a in arrays:
-        outs.append(running[at : at + a.size].reshape(a.shape))
-        at += a.size
-    return tuple(outs)
-
-
-def collected_together(array, axis):
-    leaves = jax.tree.leaves(array)
-    order = sorted(range(len(leaves)), key=lambda k: -leaves[k].size)
-    width = (1, *leaves[order[0]].shape)[-1]
-    lines = [
-        jnp.pad(leaves[k].reshape(-1), (0, -leaves[k].size % width)).reshape(-1, width)
-        for k in order
-    ]
-    both, at, found = (lax.all_gather(jnp.concatenate(lines), axis), 0, {})
-    for k, line in zip(order, lines):
-        section = both[:, at : at + len(line)].reshape(len(both), -1)
-        found[k] = section[:, : leaves[k].size].reshape(-1, *leaves[k].shape)
-        at += len(line)
-    numbers = iter(range(len(leaves)))
-    return jax.tree.map(lambda _: found[next(numbers)], array)
-
-
-def merged_by_axis(array, axes, combine):
-    for axis in axes:
-        pieces = collected_together(array, axis)
-        array = jax.tree.map(lambda part: part[0], pieces)
-        for k in range(1, lax.axis_size(axis)):
-            array = combine(array, jax.tree.map(lambda part: part[k], pieces))
-    return array
-
-
-def over_pieces(array, axis):
-    tiles = lax.all_gather(array, axis)
-    return tiles.sum(axis=0)
+def split(value, count):
+    pieces = []
+    for _ in range(count):
+        piece = lax.reduce_precision(value, 8, 7)
+        pieces.append(piece.astype(jnp.bfloat16))
+        value = value - piece
+    return pieces
 
 
 def frequencies():
@@ -85,15 +55,6 @@
     )
 
 
-def combine_parts(earlier, later):
-    shard_top = jnp.maximum(earlier[0], later[0])
-    early_factor = jnp.exp(earlier[0] - shard_top)
-    late_factor = jnp.exp(later[0] - shard_top)
-    totals = earlier[1] * early_factor + later[1] * late_factor
-    accum = earlier[2] * early_factor[..., None] + later[2] * late_factor[..., None]
-    return (shard_top, totals, accum)
-
-
 def local(
     token_input_state,
     query_matrix,
@@ -113,9 +74,13 @@
     local_cols = lax.dynamic_slice_in_dim(token_input_state, shard_index * row_count, row_count, 1)
     query_part = jnp.dot(local_cols, query_matrix, preferred_element_type=jnp.float32)
     keyval_part = jnp.dot(local_cols, key_value_weight, preferred_element_type=jnp.float32)
-    query_flat, keyval_flat = packed_total((query_part, keyval_part), SEQ)
-    query_rows = query_flat.reshape(batch_rows, kv_local, QUERY_GROUP, HEAD_SIZE)
-    key_value_rows = keyval_flat.reshape(batch_rows, kv_local, 2, HEAD_SIZE)
+    parts = jnp.concatenate(
+        [query_part.reshape(batch_rows, QUERY_GROUP, HEAD_SIZE), keyval_part.reshape(batch_rows, 2, HEAD_SIZE)], 1
+    ).reshape(batch_rows * (QUERY_GROUP + 2), HEAD_SIZE)
+    parts = copies_from(parts, SEQ[1:]).sum(0)
+    parts = exchanges(parts, SEQ[0]).reshape(batch_rows, 1, QUERY_GROUP + 2, HEAD_SIZE)
+    query_rows = parts[:, :, :QUERY_GROUP]
+    key_value_rows = parts[:, :, QUERY_GROUP:]
     columns = jnp.arange(shard_total)[None, :]
     lookup = jnp.sum(jnp.where(columns == owner_shard[:, None], live_lengths, 0), 1)
     own_length = jnp.sum(jnp.where(columns == shard_index, live_lengths, 0), 1)
@@ -149,14 +114,22 @@
         accum
         + new_prob.astype(jnp.float32)[..., None] * value_new.astype(jnp.float32)[:, :, None, :]
     )
-    overall, totals, accum = merged_by_axis((shard_top, totals, accum), SEQ, combine_parts)
+    rows = batch_rows * QUERY_GROUP
+    aux = jnp.stack(split(shard_top.reshape(rows), 3) + split(totals.reshape(rows), 2))
+    aux = jnp.pad(aux, ((0, 3), (0, HEAD_SIZE - rows)))
+    message = jnp.concatenate([accum.reshape(rows, HEAD_SIZE).astype(jnp.bfloat16), aux])
+    got = copies_from(message, SEQ)
+    aux = got[:, rows:, :rows].astype(jnp.float32)
+    tops = aux[:, 0] + aux[:, 1] + aux[:, 2]
+    weights = jnp.exp(tops - jnp.max(tops, 0))
+    totals = jnp.sum(weights * (aux[:, 3] + aux[:, 4]), 0)
+    accum = jnp.sum(weights[..., None] * got[:, :rows].astype(jnp.float32), 0)
     attended = (
-        (accum / totals[..., None])
-        .astype(jnp.bfloat16)
-        .reshape(batch_rows, kv_local * QUERY_GROUP * HEAD_SIZE)
+        (accum / totals[..., None]).astype(jnp.bfloat16).reshape(batch_rows, rows // batch_rows * HEAD_SIZE)
     )
     partial_value = jnp.dot(attended, output_weight, preferred_element_type=jnp.float32)
-    return over_pieces(partial_value, "kv").astype(jnp.bfloat16)
+    other = lax.ppermute(partial_value, "kv", ((0, 1), (1, 0)))
+    return (partial_value + other).astype(jnp.bfloat16)
 
 
 def solution(mesh):

time: 83.1 us -> 54.8 us (0.66)
  blocking collectives: 39.3 us -> 16.2 us
  waiting for transfers between devices: 19.8 us -> 9.79 us
  starting transfers between devices: 12 us -> 16.9 us
  local copies, waits for them, and re-layouts: 3.45 us -> 1.71 us
  other arithmetic: 2.77 us -> 4.46 us
    all_gather x4 -> x0, blocking collectives: 39.3 us -> none  [the longest x3 27.2 us: collected_together(): both, at, found = (lax.all_gather(jnp.concatenate(lines), axis), 0, {})]
    all_to_all x0 -> x1, blocking collectives: none -> 16.2 us  [copies_from(): lax.all_to_all(jnp.broadcast_to(array[None], (count, *array.shape)), axes...]
    all_to_all x1, waiting for transfers between devices: 19.8 us -> 6.69 us  [copies_from(): lax.all_to_all(jnp.broadcast_to(array[None], (count, *array.shape)), axes...]
    ppermute x0 -> x4, starting transfers between devices: none -> 9.34 us  [the longest x1 4.93 us: local(): other = lax.ppermute(partial_value, 'kv', ((0, 1), (1, 0)))]
    all_to_all x1, starting transfers between devices: 12 us -> 7.58 us  [copies_from(): lax.all_to_all(jnp.broadcast_to(array[None], (count, *array.shape)), axes...]
    ppermute x0 -> x4, waiting for transfers between devices: none -> 3.1 us  [the longest x1 2.27 us: exchanges(): around = lax.ppermute(array, axis, ((0, 3), (3, 0), (1, 2), (2, 1)))]
    broadcast_in_dim x1 -> x3, local copies, waits for them, and re-layouts: 1.75 us -> 0.83 us  [copies_from(): jnp.broadcast_to(array[None], (count, *array.shape))]
  transfers between devices with their start and end apart: 1 -> 5, of which waited for: 1 -> 3; matrix products, arithmetic and copies ran while one was open for 1% -> 5% of each run, Pallas kernels for 0% -> 0%
where the time goes in v1:
time: 54.8 us; the launch traced here: 54.5 us
  starting transfers between devices  16.9 us (31%)
  blocking collectives  16.2 us (30%)
  waiting for transfers between devices  9.79 us (18%)
  matrix products  5.2 us (9%)
  other arithmetic  4.46 us (8%)
  local copies, waits for them, and re-layouts  1.71 us (3%)
    all_to_all x1, blocking collectives, copies_from(): lax.all_to_all(jnp.broadcast_to(array[None], (count, *array.shape)), axes...  16.2 us
    all_to_all x1, starting transfers between devices, copies_from(): lax.all_to_all(jnp.broadcast_to(array[None], (count, *array.shape)), axes...  7.58 us
    all_to_all x1, waiting for transfers between devices, copies_from(): lax.all_to_all(jnp.broadcast_to(array[None], (count, *array.shape)), axes...  6.69 us
    ppermute x1, starting transfers between devices, local(): other = lax.ppermute(partial_value, 'kv', ((0, 1), (1, 0)))  4.93 us
    ppermute x1, starting transfers between devices, exchanges(): across = lax.ppermute(array, axis, ((0, 2), (2, 0), (1, 3), (3, 1)))  3.68 us
    ppermute x1, waiting for transfers between devices, exchanges(): around = lax.ppermute(array, axis, ((0, 3), (3, 0), (1, 2), (2, 1)))  2.27 us
    dot_general x1, matrix products, local(): jnp.einsum('bhgl,bhld->bhgd', prob_block, value_cache_rows, preferred_ele...  2.03 us
    dot_general x1, matrix products, local(): jnp.dot(local_cols, key_value_weight, preferred_element_type=jnp.float32)  1.13 us
  transfers between devices with their start and end apart: 5, of which 3 were waited for; matrix products, arithmetic and copies ran while one was open for 5% of the time, Pallas kernels for 0%

profile of v1, /device:TPU:1, one launch (start us, length us, event | category | flops | bytes accessed | tf_op | source)
XLA Modules:
  0.0 54.5 jit_solution(2160192027233535781)
XLA Ops:
  0.0 0.0 copy-start
  0.0 1.1 %fusion.37 = f32[4,256]{1,0:T(4,128)S(1)} fusion(bf16[128,256]{1,0:T(8,128)(2,1)} %param.10, bf16[4,8192]{1,0:T(4,128)(2,1)} %param.8, s32[]{:T(128)S(6)} %select_n.83), kind=kOutput, calls=%fused_computation.68 | convolution fusion | flops 262144 | bytes 70660 | tf_op jit(solution)/shard_map/dot_general | solution.py:76
  1.1 1.1 %convolution_bitcast_fusion = f32[1,4,8,128]{3,1,2,0:T(4,128)S(1)} fusion(bf16[128,1024]{1,0:T(8,128)(2,1)} %param.9, bf16[4,8192]{1,0:T(4,128)(2,1)} %param.8, s32[]{:T(128)S(6)} %select_n.83), kind=kOutput, calls=%fused_computation.6 | convolution fusion | flops 1048576 | bytes 279556 | tf_op jit(solution)/shard_map/dot_general | solution.py:75
  2.3 0.7 %broadcast_in_dim.86 = f32[16,40,128]{2,1,0:T(8,128)} broadcast(f32[40,128]{1,0:T(8,128)S(1)} %broadcast_in_dim.85), dimensions={1,2} | broadcast | bytes 348160 | tf_op jit(solution)/shard_map/broadcast_in_dim | solution.py:26
  3.0 7.6 %all-to-all-start = ((f32[16,40,128]{2,1,0:T(8,128)}), f32[16,40,128]{2,1,0:T(8,128)S(1)}, u32[]{:S(2)}, u32[]{:S(2)}) async-start(f32[16,40,128]{2,1,0:T(8,128)} %broadcast_in_dim.86), calls=%async_computation | async-start | bytes 655360 | tf_op jit(solution)/shard_map/all_to_all | solution.py:26
  10.6 0.9 %select_reduce_fusion = (s32[4]{0:T(128)S(1)}, s32[4]{0:T(128)S(1)}) fusion(s32[4,64]{1,0:T(4,128)} %param.14, s32[4]{0:T(128)} %param.15, pred[64]{0:T(512)(128)(4,1)S(1)} %iota_compare_fusion.3), kind=kLoop, calls=%fused_computation.54 | loop fusion | flops 1272 | bytes 1136 | tf_op jit(solution)/shard_map/reduce_sum | solution.py:85
  11.5 0.7 %add_convert_fusion.2 = f32[4]{0:T(128)S(1)} fusion(s32[4]{0:T(128)S(1)} %get-tuple-element.5, s32[4]{0:T(128)} %param.15), kind=kLoop, calls=%fused_computation.78 | loop fusion | flops 12 | bytes 48 | tf_op jit(solution)/shard_map/convert_element_type | solution.py:88
  12.2 0.1 iota_compare_fusion
  12.3 0.1 multiply_cosine_fusion.1
  12.4 6.7 %all-to-all-done = f32[16,40,128]{2,1,0:T(8,128)S(1)} async-done(((f32[16,40,128]{2,1,0:T(8,128)}), f32[16,40,128]{2,1,0:T(8,128)S(1)}, u32[]{:S(2)}, u32[]{:S(2)}) %all-to-all-start) | async-done | bytes 327712 | tf_op jit(solution)/shard_map/all_to_all | solution.py:26
  19.1 3.7 %collective-permute-start.2 = (f32[40,128]{1,0:T(8,128)S(1)}, f32[40,128]{1,0:T(8,128)S(1)}, u32[]{:S(2)}, u32[]{:S(2)}) collective-permute-start(f32[40,128]{1,0:T(8,128)S(1)} %reduce_sum.68), channel_id=1, source_target_pairs={{0,32},{32,0},{16,48},{48,16},{1,33},{33,1},{17,49},{49,17},{2,34}... | collective-permute-start | bytes 61448 | tf_op jit(solution)/shard_map/ppermute | solution.py:20
  22.8 0.4 collective-permute-start.1
  23.2 0.3 collective-permute-start
  23.5 0.7 %broadcast_compare_fusion = pred[4]{0:T(512)(128)(4,1)S(1)} fusion(s32[4]{0:T(128)} %param.15, s32[]{:T(128)S(6)} %add.78), kind=kLoop, calls=%fused_computation.80 | loop fusion | flops 4 | bytes 24 | tf_op jit(solution)/shard_map/eq | solution.py:97
  24.2 0.1 broadcast_in_dim.91
  24.3 0.1 broadcast_in_dim.92
  24.4 0.0 collective-permute-done.2
  24.4 2.3 %collective-permute-done.1 = f32[40,128]{1,0:T(8,128)S(1)} collective-permute-done((f32[40,128]{1,0:T(8,128)S(1)}, f32[40,128]{1,0:T(8,128)S(1)}, u32[]{:S(2)}, u32[]{:S(2)}) %collective-permute-start.1) | collective-permute-done | bytes 20512 | tf_op jit(solution)/shard_map/ppermute | solution.py:19
  26.6 0.0 collective-permute-done
  26.7 0.1 fusion.36
  26.8 0.1 maximum_convert_fusion
  26.9 0.1 subtract_convert_fusion
  27.0 0.2 multiply_reduce_fusion.1
  27.1 0.0 copy-done
  27.1 0.8 %fusion.49 = (f32[4,8]{1,0:T(4,128)S(1)}, f32[4,8,2048]{2,1,0:T(8,128)S(1)}) fusion(bf16[4,1,2048,128]{3,2,1,0:T(8,128)(2,1)S(1)} %copy-done, bf16[4,8,64]{2,1,0:T(8,128)(2,1)S(1)} %bitcast.53, bf16[4,8,64]{2,1,0:T(8,128)(2,1)S(1)} %bitcast.52, pred[4,2048]{1,0:T(4,128)(4,1)S(1)} %iota_compare_fusion), kind=kOutput, calls=%fused_computation.85 | convolution fusion | flops 16990176 | bytes 2375808 | tf_op jit(solution)/shard_map/bhgd,bhld->bhgl/dot_general | solution.py:100
  27.9 0.1 reduce_max.21
  28.0 0.1 fusion.34
  28.1 0.1 mul.231
  28.1 0.2 convert_reduce_fusion
  28.4 0.1 reduce_sum.72
  28.5 2.0 %fusion.10 = bf16[32,128]{1,0:T(8,128)(2,1)S(1)} fusion(bf16[4,1,2048,128]{3,2,1,0:T(8,128)(2,1)} %param.13, f32[4,8,2048]{2,1,0:T(8,128)S(1)} %get-tuple-element.25, f32[4,8]{1,0:T(4,128)S(1)} %get-tuple-element.15, f32[4,128]{1,0:T(4,128)S(1)} %bitcast.56, f32[4,8]{1,0:T(4,128)S(1)} %get-tuple-element.14), kind=kOutput, calls=%fused_computation.8 | convolution fusion | flops 16920576 | bytes 2369792 | tf_op jit(solution)/shard_map/bhgl,bhld->bhgd/dot_general | solution.py:108
  30.5 0.0 copy-start.1
  30.6 0.1 broadcast_in_dim.95
  30.7 16.2 %all_to_all.10 = bf16[64,40,128]{2,1,0:T(8,128)(2,1)S(1)} all-to-all(bf16[64,40,128]{2,1,0:T(8,128)(2,1)S(1)} %broadcast_in_dim.95), channel_id=1, replica_groups=mesh['kv'=2,'seq_0'=4,'seq_1'=4,'seq_2'=4,'dp'=1] {'seq_0','seq_1','seq_2'}, dimensions={0} | all-to-all | bytes 1310720 | tf_op jit(solution)/shard_map/all_to_all | solution.py:26
  46.9 0.1 copy.23
  47.1 0.1 fusion.47
  47.2 0.2 fusion.16
  47.4 0.1 div.23
  47.5 0.1 broadcast_bitcast_fusion
  47.5 0.1 copy.22
  47.6 0.4 multiply_reduce_fusion
  48.0 0.0 copy-done.1
  48.0 0.1 fusion.20
  48.1 4.9 %collective-permute-start.3 = (f32[4,128]{1,0:T(4,128)S(1)}, f32[4,128]{1,0:T(4,128)S(1)}, u32[]{:S(2)}, u32[]{:S(2)}) collective-permute-start(f32[4,128]{1,0:T(4,128)S(1)} %fusion.20), channel_id=1, source_target_pairs={{0,64},{64,0},{1,65},{65,1},{2,66},{66,2},{3,67},{67,3},{4,68},{68... | collective-permute-start | bytes 6152 | tf_op jit(solution)/shard_map/ppermute | solution.py:131
  53.1 0.8 %collective-permute-done.3 = f32[4,128]{1,0:T(4,128)S(1)} collective-permute-done((f32[4,128]{1,0:T(4,128)S(1)}, f32[4,128]{1,0:T(4,128)S(1)}, u32[]{:S(2)}, u32[]{:S(2)}) %collective-permute-start.3) | collective-permute-done | bytes 2080 | tf_op jit(solution)/shard_map/ppermute | solution.py:131
  53.9 0.6 %add_convert_fusion.1 = bf16[4,128]{1,0:T(4,128)(2,1)} fusion(f32[4,128]{1,0:T(4,128)S(1)} %fusion.20, f32[4,128]{1,0:T(4,128)S(1)} %collective-permute-done.3), kind=kLoop, calls=%fused_computation.51 | loop fusion | flops 1024 | bytes 5120 | tf_op jit(solution)/shard_map/convert_element_type | solution.py:132
  (18 shorter events, 0.2 us)
Async XLA Ops:
  0.0 27.1 %copy-start = (bf16[4,1,2048,128]{3,2,1,0:T(8,128)(2,1)S(1)}, bf16[4,1,2048,128]{3,2,1,0:T(8,128)(2,1)}, u32[]{:S(2)}) copy-start(bf16[4,1,2048,128]{3,2,1,0:T(8,128)(2,1)} %param.12) | copy-start | bytes 6291460
  3.0 16.1 %all-to-all-start = ((f32[16,40,128]{2,1,0:T(8,128)}), f32[16,40,128]{2,1,0:T(8,128)S(1)}, u32[]{:S(2)}, u32[]{:S(2)}) async-start(f32[16,40,128]{2,1,0:T(8,128)} %broadcast_in_dim.86), calls=%async_computation | async-start | bytes 655360 | tf_op jit(solution)/shard_map/all_to_all | solution.py:26
  19.1 5.2 %collective-permute-start.2 = (f32[40,128]{1,0:T(8,128)S(1)}, f32[40,128]{1,0:T(8,128)S(1)}, u32[]{:S(2)}, u32[]{:S(2)}) collective-permute-start(f32[40,128]{1,0:T(8,128)S(1)} %reduce_sum.68), channel_id=1, source_target_pairs={{0,32},{32,0},{16,48},{48,16},{1,33},{33,1},{17,49},{49,17},{2,34}... | collective-permute-start | bytes 61448 | tf_op jit(solution)/shard_map/ppermute | solution.py:20
  22.8 3.8 %collective-permute-start.1 = (f32[40,128]{1,0:T(8,128)S(1)}, f32[40,128]{1,0:T(8,128)S(1)}, u32[]{:S(2)}, u32[]{:S(2)}) collective-permute-start(f32[40,128]{1,0:T(8,128)S(1)} %reduce_sum.68), channel_id=1, source_target_pairs={{0,48},{48,0},{16,32},{32,16},{1,49},{49,1},{17,33},{33,17},{2,50}... | collective-permute-start | bytes 61448 | tf_op jit(solution)/shard_map/ppermute | solution.py:19
  23.2 3.4 %collective-permute-start = (f32[40,128]{1,0:T(8,128)S(1)}, f32[40,128]{1,0:T(8,128)S(1)}, u32[]{:S(2)}, u32[]{:S(2)}) collective-permute-start(f32[40,128]{1,0:T(8,128)S(1)} %reduce_sum.68), channel_id=1, source_target_pairs={{0,16},{16,0},{32,48},{48,32},{1,17},{17,1},{33,49},{49,33},{2,18}... | collective-permute-start | bytes 61448 | tf_op jit(solution)/shard_map/ppermute | solution.py:18
  30.5 17.5 %copy-start.1 = (bf16[1024,128]{1,0:T(8,128)(2,1)S(1)}, bf16[1024,128]{1,0:T(8,128)(2,1)}, u32[]{:S(2)}) copy-start(bf16[1024,128]{1,0:T(8,128)(2,1)} %param.11) | copy-start | bytes 786436
  48.1 5.7 %collective-permute-start.3 = (f32[4,128]{1,0:T(4,128)S(1)}, f32[4,128]{1,0:T(4,128)S(1)}, u32[]{:S(2)}, u32[]{:S(2)}) collective-permute-start(f32[4,128]{1,0:T(4,128)S(1)} %fusion.20), channel_id=1, source_target_pairs={{0,64},{64,0},{1,65},{65,1},{2,66},{66,2},{3,67},{67,3},{4,68},{68... | collective-permute-start | bytes 6152 | tf_op jit(solution)/shard_map/ppermute | solution.py:131

commit v2 on v1

v2 whole, which is shorter than its diff:
```python
import math

import jax
import jax.numpy as jnp
from jax import lax
from jax.experimental import pallas as pl
from jax.experimental.pallas import tpu as pltpu
from jax.sharding import Mesh
from jax.sharding import PartitionSpec as P

HEAD_SIZE = 128
QUERY_GROUP = 8
SEQ = ("seq_0", "seq_1", "seq_2")


rope_theta = 500000.0


def exchanges(array, axis):
    beside = lax.ppermute(array, axis, ((0, 1), (1, 0), (2, 3), (3, 2)))
    around = lax.ppermute(array, axis, ((0, 3), (3, 0), (1, 2), (2, 1)))
    across = lax.ppermute(array, axis, ((0, 2), (2, 0), (1, 3), (3, 1)))
    return beside, around, across


def held(array):
    return pltpu.with_memory_space_constraint(array, pltpu.VMEM)


def left(array):
    return pltpu.with_memory_space_constraint(array, pltpu.HBM)


def vmem():
    return pl.BlockSpec(memory_space=pltpu.VMEM)


def hbm():
    return pl.BlockSpec(memory_space=pltpu.HBM)


def smem():
    return pl.BlockSpec(memory_space=pltpu.SMEM)


def project_kernel(shard_ref, state_ref, query_ref, keyval_ref, out_ref, state_v, query_v, keyval_v, sems):
    columns = pl.ds(pl.multiple_of(shard_ref[0] * query_v.shape[0], query_v.shape[0]), query_v.shape[0])
    loads = [
        pltpu.make_async_copy(query_ref, query_v, sems.at[0]),
        pltpu.make_async_copy(keyval_ref, keyval_v, sems.at[1]),
        pltpu.make_async_copy(state_ref.at[:, columns], state_v, sems.at[2]),
    ]
    for load in loads:
        load.start()
    for load in loads:
        load.wait()
    state = state_v[...]
    parts = []
    for weights in (query_v, keyval_v):
        product = jnp.dot(state, weights[...], preferred_element_type=jnp.float32)
        parts += [product[:, at : at + HEAD_SIZE] for at in range(0, product.shape[1], HEAD_SIZE)]
    rows = jnp.concatenate(parts, 0)
    for copy in range(out_ref.shape[0]):
        out_ref[copy] = rows


def load_kernel(key_ref, value_ref, key_out, value_out, sems):
    loads = [
        pltpu.make_async_copy(key_ref, key_out, sems.at[0]),
        pltpu.make_async_copy(value_ref, value_out, sems.at[1]),
    ]
    for load in loads:
        load.start()
    for load in loads:
        load.wait()


def attend_kernel(
    length_ref, owner_ref, own_ref, beside_ref, around_ref, across_ref, cosine_ref, sine_ref,
    key_ref, value_ref, out_ref, score_ref,
):
    total = (own_ref[...] + beside_ref[...]) + (around_ref[...] + across_ref[...])
    turned = total * cosine_ref[...] + pltpu.roll(total, HEAD_SIZE // 2, 1) * sine_ref[...]
    score_ref[0 : total.shape[0], 0:HEAD_SIZE] = turned
    batch, _, slots, _ = key_ref.shape
    scaling = 1.0 / math.sqrt(HEAD_SIZE)
    lane = lax.broadcasted_iota(jnp.int32, (QUERY_GROUP, HEAD_SIZE), 1)
    sublane = lax.broadcasted_iota(jnp.int32, (QUERY_GROUP, HEAD_SIZE), 0)
    top_row = jnp.zeros((1, HEAD_SIZE), jnp.float32)
    total_row = jnp.zeros((1, HEAD_SIZE), jnp.float32)
    picks = []
    for b in range(batch):
        query = score_ref[pl.ds(b, QUERY_GROUP, stride=batch), 0:HEAD_SIZE].astype(jnp.bfloat16)
        key_new = turned[QUERY_GROUP * batch + b :][:1].astype(jnp.bfloat16)
        value_new = turned[(QUERY_GROUP + 1) * batch + b :][:1].astype(jnp.bfloat16)
        picks.append((query, key_new.astype(jnp.float32), value_new.astype(jnp.float32)))
    slot = lax.broadcasted_iota(jnp.int32, (QUERY_GROUP, slots), 1)
    accums = []
    for b, (query, key_new, value_new) in enumerate(picks):
        scores = (
            lax.dot_general(
                query, key_ref[b, 0], (((1,), (1,)), ((), ())), preferred_element_type=jnp.float32
            )
            * scaling
        )
        scores = jnp.where(slot < length_ref[b], scores, -jnp.inf)
        new_score = jnp.sum(query.astype(jnp.float32) * key_new, -1, keepdims=True) * scaling
        owns = owner_ref[b] > 0
        top = jnp.maximum(jnp.max(scores, -1, keepdims=True), jnp.where(owns, new_score, -jnp.inf))
        prob = jnp.exp(scores - top).astype(jnp.bfloat16)
        new_prob = jnp.where(owns, jnp.exp(new_score - top), 0.0).astype(jnp.bfloat16).astype(jnp.float32)
        weight = jnp.sum(prob.astype(jnp.float32), -1, keepdims=True) + new_prob
        accum = jnp.dot(prob, value_ref[b, 0], preferred_element_type=jnp.float32) + new_prob * value_new
        accums.append(accum)
        mine = lane == sublane + b * QUERY_GROUP
        top_row += jnp.sum(jnp.where(mine, top, 0.0), 0, keepdims=True)
        total_row += jnp.sum(jnp.where(mine, weight, 0.0), 0, keepdims=True)
    side = jnp.zeros((QUERY_GROUP, HEAD_SIZE), jnp.float32)
    at = 0
    for row, count in ((top_row, 3), (total_row, 2)):
        for _ in range(count):
            piece = row.astype(jnp.bfloat16).astype(jnp.float32)
            side = jnp.where(sublane == at, piece, side)
            row = row - piece
            at += 1
    message = jnp.concatenate(accums + [side], 0).astype(jnp.bfloat16)
    for copy in range(out_ref.shape[0]):
        out_ref[copy] = message


def frequencies():
    exponent = jnp.arange(0, HEAD_SIZE, 2).astype(jnp.float32) / HEAD_SIZE
    return jnp.power(rope_theta, -exponent)


def local(
    token_input_state,
    query_matrix,
    key_value_weight,
    output_weight,
    key_cache_rows,
    value_cache_rows,
    live_lengths,
    owner_shard,
):
    batch_rows = token_input_state.shape[0]
    slot_count = key_cache_rows.shape[2]
    row_count = query_matrix.shape[0]
    shard_index = lax.axis_index(SEQ)
    shard_total = lax.axis_size(SEQ)
    heads = QUERY_GROUP + 2
    rows = batch_rows * heads
    copies = pl.pallas_call(
        project_kernel,
        out_shape=pltpu.VMEM((lax.axis_size(SEQ[1:]), rows, HEAD_SIZE), jnp.float32),
        in_specs=[smem(), hbm(), hbm(), hbm()],
        out_specs=vmem(),
        scratch_shapes=[
            pltpu.VMEM((batch_rows, row_count), jnp.bfloat16),
            pltpu.VMEM(query_matrix.shape, jnp.bfloat16),
            pltpu.VMEM(key_value_weight.shape, jnp.bfloat16),
            pltpu.SemaphoreType.DMA((3,)),
        ],
        compiler_params=pltpu.CompilerParams(vmem_limit_bytes=8 << 20),
        name="project",
    )(shard_index.reshape(1), left(token_input_state), left(query_matrix), left(key_value_weight))
    parts = lax.all_to_all(copies, SEQ[1:], 0, 0, tiled=True).sum(0)
    beside, around, across = exchanges(parts, SEQ[0])
    columns = jnp.arange(shard_total)[None, :]
    lookup = jnp.sum(jnp.where(columns == owner_shard[:, None], live_lengths, 0), 1)
    own_length = jnp.sum(jnp.where(columns == shard_index, live_lengths, 0), 1)
    position = owner_shard * slot_count + lookup
    angles = position.astype(jnp.float32)[:, None] * frequencies()[None, :]
    cosine, sine = jnp.cos(angles), jnp.sin(angles)
    one, zero = jnp.ones_like(angles), jnp.zeros_like(angles)
    cosine = jnp.concatenate([cosine, cosine], 1)
    sine = jnp.concatenate([-sine, sine], 1)
    straight = jnp.concatenate([one, one], 1)
    cosine = jnp.concatenate([cosine] * (heads - 1) + [straight], 0)
    sine = jnp.concatenate([sine] * (heads - 1) + [jnp.zeros_like(straight)], 0)
    is_owner = (owner_shard == shard_index).astype(jnp.int32)
    count = batch_rows * QUERY_GROUP
    keys, values = pl.pallas_call(
        load_kernel,
        out_shape=[pltpu.VMEM(a.shape, a.dtype) for a in (key_cache_rows, value_cache_rows)],
        in_specs=[hbm(), hbm()],
        out_specs=[vmem(), vmem()],
        scratch_shapes=[pltpu.SemaphoreType.DMA((2,))],
        compiler_params=pltpu.CompilerParams(vmem_limit_bytes=8 << 20),
        name="load",
    )(left(key_cache_rows), left(value_cache_rows))
    message = pl.pallas_call(
        attend_kernel,
        out_shape=pltpu.VMEM((shard_total, count + QUERY_GROUP, HEAD_SIZE), jnp.bfloat16),
        in_specs=[smem(), smem()] + [vmem()] * 8,
        out_specs=vmem(),
        scratch_shapes=[pltpu.VMEM((rows, HEAD_SIZE), jnp.float32)],
        compiler_params=pltpu.CompilerParams(vmem_limit_bytes=8 << 20),
        name="attend",
    )(
        own_length,
        is_owner,
        *(held(a) for a in (parts, beside, around, across, cosine, sine, keys, values)),
    )
    got = lax.all_to_all(message, SEQ, 0, 0, tiled=True)
    aux = got[:, count:, :count].astype(jnp.float32)
    tops = aux[:, 0] + aux[:, 1] + aux[:, 2]
    weights = jnp.exp(tops - jnp.max(tops, 0))
    totals = jnp.sum(weights * (aux[:, 3] + aux[:, 4]), 0)
    accum = jnp.sum(weights[..., None] * got[:, :count].astype(jnp.float32), 0)
    attended = (accum / totals[..., None]).astype(jnp.bfloat16).reshape(batch_rows, QUERY_GROUP * HEAD_SIZE)
    partial_value = jnp.dot(attended, output_weight, preferred_element_type=jnp.float32)
    other = lax.ppermute(partial_value, "kv", ((0, 1), (1, 0)))
    return (partial_value + other).astype(jnp.bfloat16)


def solution(mesh):
    finer = Mesh(
        mesh.devices.reshape(mesh.shape["kv"], 4, 4, 4, mesh.shape["dp"]),
        ("kv", "seq_0", "seq_1", "seq_2", "dp"),
    )
    return jax.shard_map(
        local,
        mesh=finer,
        in_specs=(
            P("dp", None),
            P(SEQ, "kv"),
            P(SEQ, "kv"),
            P("kv", SEQ),
            P("dp", "kv", SEQ, None),
            P("dp", "kv", SEQ, None),
            P("dp", None),
            P("dp"),
        ),
        out_specs=P("dp", SEQ),
        check_vma=False,
    )
```

time: 54.8 us -> 51.8 us (0.945)
  Pallas kernels: 0 us -> 6.44 us
  matrix products: 5.2 us -> 0.15 us
  waiting for transfers between devices: 9.79 us -> 7.5 us
  local copies, waits for them, and re-layouts: 1.71 us -> 0.38 us
  blocking collectives: 16.2 us -> 17.5 us
  starting transfers between devices: 16.9 us -> 15.9 us
  other arithmetic: 4.46 us -> 3.54 us
    pallas_call x0 -> x3, Pallas kernels: none -> 6.44 us  [the longest x1 2.3 us: local(): pl.pallas_call(attend_kernel, out_shape=pltpu.VMEM((shard_total, count +...]
    dot_general x4 -> x0, matrix products: 5.05 us -> none  [the longest x1 2.03 us: local(): jnp.einsum('bhgl,bhld->bhgd', prob_block, value_cache_rows, preferred_ele...]
    ppermute x1, waiting for transfers between devices: 2.27 us -> 0.56 us  [exchanges(): around = lax.ppermute(array, axis, ((0, 3), (3, 0), (1, 2), (2, 1)))]
    all_to_all x1, blocking collectives: 16.2 us -> 17.5 us  [local(): got = lax.all_to_all(message, SEQ, 0, 0, tiled=True)]
    ppermute x1, starting transfers between devices: 4.93 us -> 3.92 us  [local(): other = lax.ppermute(partial_value, 'kv', ((0, 1), (1, 0)))]
    broadcast_in_dim x5 -> x1, local copies, waits for them, and re-layouts: 0.99 us -> 0.01 us  [local(): sine = jnp.concatenate([sine] * (heads - 1) + [jnp.zeros_like(straight)], 0)]
    eq x1 -> x0, other arithmetic: 0.66 us -> none  [local(): is_owner = (owner_shard == shard_index)[:, None, None]]
    all_to_all x1, waiting for transfers between devices: 6.69 us -> 6.11 us  [local(): parts = lax.all_to_all(copies, SEQ[1:], 0, 0, tiled=True).sum(0)]
  transfers between devices with their start and end apart: 5 -> 5, of which waited for: 3 -> 3; matrix products, arithmetic and copies ran while one was open for 5% -> 5% of each run, Pallas kernels for 0% -> 4%
where the time goes in v2:
time: 51.8 us; the launch traced here: 51.5 us
  blocking collectives  17.5 us (34%)
  starting transfers between devices  15.9 us (31%)
  waiting for transfers between devices  7.5 us (14%)
  Pallas kernels  6.44 us (12%)
  other arithmetic  3.54 us (7%)
    all_to_all x1, blocking collectives, local(): got = lax.all_to_all(message, SEQ, 0, 0, tiled=True)  17.5 us
    all_to_all x1, starting transfers between devices, local(): parts = lax.all_to_all(copies, SEQ[1:], 0, 0, tiled=True).sum(0)  7.6 us
    all_to_all x1, waiting for transfers between devices, local(): parts = lax.all_to_all(copies, SEQ[1:], 0, 0, tiled=True).sum(0)  6.11 us
    ppermute x1, starting transfers between devices, local(): other = lax.ppermute(partial_value, 'kv', ((0, 1), (1, 0)))  3.92 us
    ppermute x1, starting transfers between devices, exchanges(): across = lax.ppermute(array, axis, ((0, 2), (2, 0), (1, 3), (3, 1)))  3.68 us
    pallas_call x1, Pallas kernels, local(): pl.pallas_call(attend_kernel, out_shape=pltpu.VMEM((shard_total, count +...  2.3 us
    pallas_call x1, Pallas kernels, local(): pl.pallas_call(load_kernel, out_shape=[pltpu.VMEM(a.shape, a.dtype) for a...  2.24 us
    pallas_call x1, Pallas kernels, local(): pl.pallas_call(project_kernel, out_shape=pltpu.VMEM((lax.axis_size(SEQ[1:...  1.9 us
  transfers between devices with their start and end apart: 5, of which 3 were waited for; matrix products, arithmetic and copies ran while one was open for 5% of the time, Pallas kernels for 4%

profile of v2, /device:TPU:1, one launch (start us, length us, event | category | flops | bytes accessed | tf_op | source)
XLA Modules:
  0.0 51.5 jit_solution(324044424363983356)
XLA Ops:
  0.0 0.0 copy-start
  0.0 1.9 %project.1 = f32[16,40,128]{2,1,0:T(8,128)} custom-call(s32[1]{0:T(128)} %bitcast.shard_ref, bf16[4,8192]{1,0:T(4,128)(2,1)} %state_ref.1, bf16[128,1024]{1,0:T(8,128)(2,1)} %query_ref.1, bf16[128,256]{1,0:T(8,128)(2,1)} %keyval_ref.1), custom_call_target="tpu_custom_call" | custom-call | tf_op jit(solution)/shard_map/project/pallas_call | solution.py:153
  1.9 7.6 %all-to-all-start = ((f32[16,40,128]{2,1,0:T(8,128)}), f32[16,40,128]{2,1,0:T(8,128)S(1)}, u32[]{:S(2)}, u32[]{:S(2)}) async-start(f32[16,40,128]{2,1,0:T(8,128)} %project.1), calls=%async_computation | async-start | bytes 655360 | tf_op jit(solution)/shard_map/all_to_all | solution.py:167
  9.5 0.7 %compare_convert_fusion.owner_ref = s32[4]{0:T(128)S(1)} fusion(s32[4]{0:T(128)} %param.15, s32[]{:T(128)} %add.37), kind=kLoop, calls=%fused_computation.19 | loop fusion | flops 8 | bytes 36 | tf_op jit(solution)/shard_map/convert_element_type | solution.py:181
  10.2 0.9 %select_reduce_fusion = (s32[4]{0:T(128)S(1)}, s32[4]{0:T(128)S(1)}) fusion(s32[4,64]{1,0:T(4,128)} %param.14, s32[4]{0:T(128)} %param.15, pred[64]{0:T(512)(128)(4,1)S(1)} %iota_compare_fusion.1), kind=kLoop, calls=%fused_computation.16 | loop fusion | flops 1272 | bytes 1136 | tf_op jit(solution)/shard_map/reduce_sum | solution.py:170
  11.1 0.7 %add_convert_fusion.1 = f32[4]{0:T(128)S(1)} fusion(s32[4]{0:T(128)S(1)} %get-tuple-element.9, s32[4]{0:T(128)} %param.15), kind=kLoop, calls=%fused_computation.21 | loop fusion | flops 12 | bytes 48 | tf_op jit(solution)/shard_map/convert_element_type | solution.py:173
  11.8 0.1 fusion.4
  11.9 6.1 %all-to-all-done = f32[16,40,128]{2,1,0:T(8,128)S(1)} async-done(((f32[16,40,128]{2,1,0:T(8,128)}), f32[16,40,128]{2,1,0:T(8,128)S(1)}, u32[]{:S(2)}, u32[]{:S(2)}) %all-to-all-start) | async-done | bytes 327712 | tf_op jit(solution)/shard_map/all_to_all | solution.py:167
  18.0 3.7 %collective-permute-start.2 = (f32[40,128]{1,0:T(8,128)S(1)}, f32[40,128]{1,0:T(8,128)S(1)}, u32[]{:S(2)}, u32[]{:S(2)}) collective-permute-start(f32[40,128]{1,0:T(8,128)S(1)} %reduce_sum.48.own_ref), channel_id=1, source_target_pairs={{0,32},{32,0},{16,48},{48,16},{1,33},{33,1},{17,49},{49,17},{2,34}... | collective-permute-start | bytes 61448 | tf_op jit(solution)/shard_map/ppermute | solution.py:22
  21.7 0.4 collective-permute-start.1
  22.1 0.3 collective-permute-start
  22.4 0.1 pad_maximum_fusion
  22.5 0.1 concatenate.17.cosine_ref
  22.6 0.1 concatenate.19.sine_ref
  22.7 2.2 %load.1 = (bf16[4,1,2048,128]{3,2,1,0:T(8,128)(2,1)S(1)}, bf16[4,1,2048,128]{3,2,1,0:T(8,128)(2,1)S(1)}) custom-call(bf16[4,1,2048,128]{3,2,1,0:T(8,128)(2,1)} %key_ref.1, bf16[4,1,2048,128]{3,2,1,0:T(8,128)(2,1)} %value_ref.1), custom_call_target="tpu_custom_call" | custom-call | tf_op jit(solution)/shard_map/load/pallas_call | solution.py:183
  25.0 0.0 collective-permute-done.2.across_ref
  25.0 0.6 %collective-permute-done.1.around_ref = f32[40,128]{1,0:T(8,128)S(1)} collective-permute-done((f32[40,128]{1,0:T(8,128)S(1)}, f32[40,128]{1,0:T(8,128)S(1)}, u32[]{:S(2)}, u32[]{:S(2)}) %collective-permute-start.1) | collective-permute-done | bytes 20512 | tf_op jit(solution)/shard_map/ppermute | solution.py:21
  25.5 0.0 collective-permute-done.beside_ref
  25.5 2.3 %attend.1 = bf16[64,40,128]{2,1,0:T(8,128)(2,1)S(1)} custom-call(s32[4]{0:T(128)S(1)} %get-tuple-element.10.length_ref, s32[4]{0:T(128)S(1)} %compare_convert_fusion.owner_ref, f32[40,128]{1,0:T(8,128)S(1)} %reduce_sum.48.own_ref, f32[40,128]{1,0:T(8,128)S(1)} %collective-permute-done.beside_ref, f32[40,128]{1,0:T(8,128)S(1)} %collective-permute-done.1.around_ref, ...), custom_call_target="tpu_custom_call" | custom-call | tf_op jit(solution)/shard_map/attend/pallas_call | solution.py:192
  27.8 17.5 %all_to_all.10 = bf16[64,40,128]{2,1,0:T(8,128)(2,1)S(1)} all-to-all(bf16[64,40,128]{2,1,0:T(8,128)(2,1)S(1)} %attend.1), channel_id=1, replica_groups=mesh['kv'=2,'seq_0'=4,'seq_1'=4,'seq_2'=4,'dp'=1] {'seq_0','seq_1','seq_2'}, dimensions={0} | all-to-all | bytes 1310720 | tf_op jit(solution)/shard_map/all_to_all | solution.py:205
  45.4 0.1 fusion.7
  45.6 0.3 multiply_reduce_fusion
  45.9 0.1 div.21
  46.0 0.1 broadcast_bitcast_fusion
  46.1 0.0 copy-done
  46.1 0.1 fusion.2
  46.2 3.9 %collective-permute-start.3 = (f32[4,128]{1,0:T(4,128)S(1)}, f32[4,128]{1,0:T(4,128)S(1)}, u32[]{:S(2)}, u32[]{:S(2)}) collective-permute-start(f32[4,128]{1,0:T(4,128)S(1)} %fusion.2), channel_id=1, source_target_pairs={{0,64},{64,0},{1,65},{65,1},{2,66},{66,2},{3,67},{67,3},{4,68},{68... | collective-permute-start | bytes 6152 | tf_op jit(solution)/shard_map/ppermute | solution.py:213
  50.1 0.8 %collective-permute-done.3 = f32[4,128]{1,0:T(4,128)S(1)} collective-permute-done((f32[4,128]{1,0:T(4,128)S(1)}, f32[4,128]{1,0:T(4,128)S(1)}, u32[]{:S(2)}, u32[]{:S(2)}) %collective-permute-start.3) | collective-permute-done | bytes 2080 | tf_op jit(solution)/shard_map/ppermute | solution.py:213
  51.0 0.6 %add_convert_fusion = bf16[4,128]{1,0:T(4,128)(2,1)} fusion(f32[4,128]{1,0:T(4,128)S(1)} %fusion.2, f32[4,128]{1,0:T(4,128)S(1)} %collective-permute-done.3), kind=kLoop, calls=%fused_computation.15 | loop fusion | flops 1024 | bytes 5120 | tf_op jit(solution)/shard_map/convert_element_type | solution.py:214
  (9 shorter events, 0.1 us)
Async XLA Ops:
  0.0 46.1 %copy-start = (bf16[1024,128]{1,0:T(8,128)(2,1)S(1)}, bf16[1024,128]{1,0:T(8,128)(2,1)}, u32[]{:S(2)}) copy-start(bf16[1024,128]{1,0:T(8,128)(2,1)} %param.11) | copy-start | bytes 786436
  1.9 16.1 %all-to-all-start = ((f32[16,40,128]{2,1,0:T(8,128)}), f32[16,40,128]{2,1,0:T(8,128)S(1)}, u32[]{:S(2)}, u32[]{:S(2)}) async-start(f32[16,40,128]{2,1,0:T(8,128)} %project.1), calls=%async_computation | async-start | bytes 655360 | tf_op jit(solution)/shard_map/all_to_all | solution.py:167
  18.0 7.0 %collective-permute-start.2 = (f32[40,128]{1,0:T(8,128)S(1)}, f32[40,128]{1,0:T(8,128)S(1)}, u32[]{:S(2)}, u32[]{:S(2)}) collective-permute-start(f32[40,128]{1,0:T(8,128)S(1)} %reduce_sum.48.own_ref), channel_id=1, source_target_pairs={{0,32},{32,0},{16,48},{48,16},{1,33},{33,1},{17,49},{49,17},{2,34}... | collective-permute-start | bytes 61448 | tf_op jit(solution)/shard_map/ppermute | solution.py:22
  21.7 3.8 %collective-permute-start.1 = (f32[40,128]{1,0:T(8,128)S(1)}, f32[40,128]{1,0:T(8,128)S(1)}, u32[]{:S(2)}, u32[]{:S(2)}) collective-permute-start(f32[40,128]{1,0:T(8,128)S(1)} %reduce_sum.48.own_ref), channel_id=1, source_target_pairs={{0,48},{48,0},{16,32},{32,16},{1,49},{49,1},{17,33},{33,17},{2,50}... | collective-permute-start | bytes 61448 | tf_op jit(solution)/shard_map/ppermute | solution.py:21
  22.1 3.4 %collective-permute-start = (f32[40,128]{1,0:T(8,128)S(1)}, f32[40,128]{1,0:T(8,128)S(1)}, u32[]{:S(2)}, u32[]{:S(2)}) collective-permute-start(f32[40,128]{1,0:T(8,128)S(1)} %reduce_sum.48.own_ref), channel_id=1, source_target_pairs={{0,16},{16,0},{32,48},{48,32},{1,17},{17,1},{33,49},{49,33},{2,18}... | collective-permute-start | bytes 61448 | tf_op jit(solution)/shard_map/ppermute | solution.py:20
  46.2 4.7 %collective-permute-start.3 = (f32[4,128]{1,0:T(4,128)S(1)}, f32[4,128]{1,0:T(4,128)S(1)}, u32[]{:S(2)}, u32[]{:S(2)}) collective-permute-start(f32[4,128]{1,0:T(4,128)S(1)} %fusion.2), channel_id=1, source_target_pairs={{0,64},{64,0},{1,65},{65,1},{2,66},{66,2},{3,67},{67,3},{4,68},{68... | collective-permute-start | bytes 6152 | tf_op jit(solution)/shard_map/ppermute | solution.py:213

commit v3 on v2

--- a/solution.py
+++ b/solution.py
@@ -64,25 +64,50 @@
         out_ref[copy] = rows
 
 
-def load_kernel(key_ref, value_ref, key_out, value_out, sems):
-    loads = [
-        pltpu.make_async_copy(key_ref, key_out, sems.at[0]),
-        pltpu.make_async_copy(value_ref, value_out, sems.at[1]),
-    ]
+def prepare_kernel(
+    shard_ref, live_ref, owner_ref, rate_ref, key_ref, value_ref, output_ref,
+    key_out, value_out, output_out, cosine_ref, sine_ref, own_ref, sems,
+):
+    batch, _, slots, _ = key_ref.shape
+    loads = [pltpu.make_async_copy(output_ref, output_out, sems.at[2 * batch])]
+    for b in range(batch):
+        loads.append(pltpu.make_async_copy(key_ref.at[b], key_out.at[b], sems.at[b]))
+        loads.append(pltpu.make_async_copy(value_ref.at[b], value_out.at[b], sems.at[batch + b]))
     for load in loads:
         load.start()
+    sublane = lax.broadcasted_iota(jnp.int32, (2 * batch, HEAD_SIZE), 0)
+    lane = lax.broadcasted_iota(jnp.int32, (2 * batch, HEAD_SIZE), 1)
+    place = jnp.zeros((2 * batch, HEAD_SIZE), jnp.int32)
+    own = place
+    for b in range(batch):
+        position = owner_ref[b] * slots + live_ref[b, owner_ref[b]]
+        place = jnp.where(sublane % batch == b, position, place)
+        own = jnp.where(sublane == b, live_ref[b, shard_ref[0]], own)
+        own = jnp.where(sublane == b + batch, jnp.where(owner_ref[b] == shard_ref[0], 1, 0), own)
+    own_ref[...] = own
+    angle = place.astype(jnp.float32) * rate_ref[...]
+    cosine_ref[...] = jnp.cos(angle)
+    sine = jnp.sin(angle)
+    sine_ref[...] = jnp.where(lane < HEAD_SIZE // 2, -sine, sine)
     for load in loads:
         load.wait()
 
 
 def attend_kernel(
-    length_ref, owner_ref, own_ref, beside_ref, around_ref, across_ref, cosine_ref, sine_ref,
+    part_ref, beside_ref, around_ref, across_ref, cosine_ref, sine_ref, own_ref,
     key_ref, value_ref, out_ref, score_ref,
 ):
-    total = (own_ref[...] + beside_ref[...]) + (around_ref[...] + across_ref[...])
-    turned = total * cosine_ref[...] + pltpu.roll(total, HEAD_SIZE // 2, 1) * sine_ref[...]
-    score_ref[0 : total.shape[0], 0:HEAD_SIZE] = turned
     batch, _, slots, _ = key_ref.shape
+    cosine, sine = cosine_ref[...], sine_ref[...]
+    straight = lax.broadcasted_iota(jnp.int32, cosine.shape, 0) >= batch
+    for at in range(0, score_ref.shape[0], 2 * batch):
+        tile = pl.ds(at, 2 * batch)
+        total = (part_ref[tile, :] + beside_ref[tile, :]) + (around_ref[tile, :] + across_ref[tile, :])
+        if at + 2 * batch == score_ref.shape[0]:
+            cosine = jnp.where(straight, 1.0, cosine)
+            sine = jnp.where(straight, 0.0, sine)
+        turned = total * cosine + pltpu.roll(total, HEAD_SIZE // 2, 1) * sine
+        score_ref[tile, :] = turned
     scaling = 1.0 / math.sqrt(HEAD_SIZE)
     lane = lax.broadcasted_iota(jnp.int32, (QUERY_GROUP, HEAD_SIZE), 1)
     sublane = lax.broadcasted_iota(jnp.int32, (QUERY_GROUP, HEAD_SIZE), 0)
@@ -90,9 +115,9 @@
     total_row = jnp.zeros((1, HEAD_SIZE), jnp.float32)
     picks = []
     for b in range(batch):
-        query = score_ref[pl.ds(b, QUERY_GROUP, stride=batch), 0:HEAD_SIZE].astype(jnp.bfloat16)
-        key_new = turned[QUERY_GROUP * batch + b :][:1].astype(jnp.bfloat16)
-        value_new = turned[(QUERY_GROUP + 1) * batch + b :][:1].astype(jnp.bfloat16)
+        query = score_ref[pl.ds(b, QUERY_GROUP, stride=batch), :].astype(jnp.bfloat16)
+        key_new = turned[b : b + 1].astype(jnp.bfloat16)
+        value_new = turned[batch + b : batch + b + 1].astype(jnp.bfloat16)
         picks.append((query, key_new.astype(jnp.float32), value_new.astype(jnp.float32)))
     slot = lax.broadcasted_iota(jnp.int32, (QUERY_GROUP, slots), 1)
     accums = []
@@ -103,9 +128,9 @@
             )
             * scaling
         )
-        scores = jnp.where(slot < length_ref[b], scores, -jnp.inf)
+        scores = jnp.where(slot < own_ref[b : b + 1, 0:1], scores, -jnp.inf)
         new_score = jnp.sum(query.astype(jnp.float32) * key_new, -1, keepdims=True) * scaling
-        owns = owner_ref[b] > 0
+        owns = own_ref[batch + b : batch + b + 1, 0:1] > 0
         top = jnp.maximum(jnp.max(scores, -1, keepdims=True), jnp.where(owns, new_score, -jnp.inf))
         prob = jnp.exp(scores - top).astype(jnp.bfloat16)
         new_prob = jnp.where(owns, jnp.exp(new_score - top), 0.0).astype(jnp.bfloat16).astype(jnp.float32)
@@ -128,6 +153,64 @@
         out_ref[copy] = message
 
 
+def merge_kernel(got_ref, output_ref, out_ref):
+    sources = got_ref.shape[0]
+    batch = out_ref.shape[0]
+    count = batch * QUERY_GROUP
+    side = got_ref[:, count:, :].astype(jnp.float32).reshape(sources * QUERY_GROUP, HEAD_SIZE).astype(jnp.bfloat16)
+    source = lax.broadcasted_iota(jnp.int32, (HEAD_SIZE, sources * QUERY_GROUP), 0)
+    entry = lax.broadcasted_iota(jnp.int32, (HEAD_SIZE, sources * QUERY_GROUP), 1)
+    place = entry - source * QUERY_GROUP
+
+    def gathered(low, high):
+        chosen = ((place >= low) & (place < high)).astype(jnp.float32).astype(jnp.bfloat16)
+        return jnp.dot(chosen, side, preferred_element_type=jnp.float32).T[:count]
+
+    there = lax.broadcasted_iota(jnp.int32, (count, HEAD_SIZE), 1) < sources
+    tops = jnp.where(there, gathered(0, 3), -jnp.inf)
+    weights = jnp.exp(tops - jnp.max(tops, -1, keepdims=True))
+    total = jnp.sum(weights * gathered(3, 5), -1, keepdims=True)
+    accum = jnp.zeros((count, HEAD_SIZE), jnp.float32)
+    for at in range(sources):
+        accum += weights[:, at : at + 1] * got_ref[at, :count, :].astype(jnp.float32)
+    attended = accum / total
+    head = lax.broadcasted_iota(jnp.int32, (count, HEAD_SIZE), 0) % QUERY_GROUP
+    spread = jnp.concatenate(
+        [jnp.where(head == at, attended, 0.0).astype(jnp.bfloat16) for at in range(QUERY_GROUP)], 1
+    )
+    product = jnp.dot(spread, output_ref[...], preferred_element_type=jnp.float32)
+    out_ref[...] = jnp.sum(product.reshape(batch, QUERY_GROUP, HEAD_SIZE), 1)
+
+
+def merge_kernel(got_ref, output_ref, out_ref):
+    sources = got_ref.shape[0]
+    batch = out_ref.shape[0]
+    count = batch * QUERY_GROUP
+    side = got_ref[:, count:, :].astype(jnp.float32).reshape(sources * QUERY_GROUP, HEAD_SIZE).astype(jnp.bfloat16)
+    source = lax.broadcasted_iota(jnp.int32, (HEAD_SIZE, sources * QUERY_GROUP), 0)
+    entry = lax.broadcasted_iota(jnp.int32, (HEAD_SIZE, sources * QUERY_GROUP), 1)
+    place = entry - source * QUERY_GROUP
+
+    def gathered(low, high):
+        chosen = ((place >= low) & (place < high)).astype(jnp.float32).astype(jnp.bfloat16)
+        return jnp.dot(chosen, side, preferred_element_type=jnp.float32).T[:count]
+
+    there = lax.broadcasted_iota(jnp.int32, (count, HEAD_SIZE), 1) < sources
+    tops = jnp.where(there, gathered(0, 3), -jnp.inf)
+    weights = jnp.exp(tops - jnp.max(tops, -1, keepdims=True))
+    total = jnp.sum(weights * gathered(3, 5), -1, keepdims=True)
+    accum = jnp.zeros((count, HEAD_SIZE), jnp.float32)
+    for at in range(sources):
+        accum += weights[:, at : at + 1] * got_ref[at, :count, :].astype(jnp.float32)
+    attended = accum / total
+    head = lax.broadcasted_iota(jnp.int32, (count, HEAD_SIZE), 0) % QUERY_GROUP
+    spread = jnp.concatenate(
+        [jnp.where(head == at, attended, 0.0).astype(jnp.bfloat16) for at in range(QUERY_GROUP)], 1
+    )
+    product = jnp.dot(spread, output_ref[...], preferred_element_type=jnp.float32)
+    out_ref[...] = jnp.sum(product.reshape(batch, QUERY_GROUP, HEAD_SIZE), 1)
+
+
 def frequencies():
     exponent = jnp.arange(0, HEAD_SIZE, 2).astype(jnp.float32) / HEAD_SIZE
     return jnp.power(rope_theta, -exponent)
@@ -144,12 +227,14 @@
     owner_shard,
 ):
     batch_rows = token_input_state.shape[0]
-    slot_count = key_cache_rows.shape[2]
     row_count = query_matrix.shape[0]
     shard_index = lax.axis_index(SEQ)
-    shard_total = lax.axis_size(SEQ)
     heads = QUERY_GROUP + 2
     rows = batch_rows * heads
+    exponent = jnp.arange(0, HEAD_SIZE, 2).astype(jnp.float32) / HEAD_SIZE
+    rates = jnp.power(rope_theta, -exponent)
+    rates = jnp.concatenate([rates, rates]).reshape(1, HEAD_SIZE)
+    index, rates = lax.optimization_barrier((shard_index.reshape(1), rates))
     copies = pl.pallas_call(
         project_kernel,
         out_shape=pltpu.VMEM((lax.axis_size(SEQ[1:]), rows, HEAD_SIZE), jnp.float32),
@@ -163,53 +248,50 @@
         ],
         compiler_params=pltpu.CompilerParams(vmem_limit_bytes=8 << 20),
         name="project",
-    )(shard_index.reshape(1), left(token_input_state), left(query_matrix), left(key_value_weight))
-    parts = lax.all_to_all(copies, SEQ[1:], 0, 0, tiled=True).sum(0)
+    )(index, left(token_input_state), left(query_matrix), left(key_value_weight))
+    got = lax.all_to_all(copies, SEQ[1:], 0, 0, tiled=True)
+    got, later_index, rates = lax.optimization_barrier((got, index, rates))
+    parts = got.sum(0)
     beside, around, across = exchanges(parts, SEQ[0])
-    columns = jnp.arange(shard_total)[None, :]
-    lookup = jnp.sum(jnp.where(columns == owner_shard[:, None], live_lengths, 0), 1)
-    own_length = jnp.sum(jnp.where(columns == shard_index, live_lengths, 0), 1)
-    position = owner_shard * slot_count + lookup
-    angles = position.astype(jnp.float32)[:, None] * frequencies()[None, :]
-    cosine, sine = jnp.cos(angles), jnp.sin(angles)
-    one, zero = jnp.ones_like(angles), jnp.zeros_like(angles)
-    cosine = jnp.concatenate([cosine, cosine], 1)
-    sine = jnp.concatenate([-sine, sine], 1)
-    straight = jnp.concatenate([one, one], 1)
-    cosine = jnp.concatenate([cosine] * (heads - 1) + [straight], 0)
-    sine = jnp.concatenate([sine] * (heads - 1) + [jnp.zeros_like(straight)], 0)
-    is_owner = (owner_shard == shard_index).astype(jnp.int32)
+    caches = (key_cache_rows, value_cache_rows, output_weight)
+    table = pltpu.VMEM((2 * batch_rows, HEAD_SIZE), jnp.float32)
+    places = pltpu.VMEM((2 * batch_rows, HEAD_SIZE), jnp.int32)
+    keys, values, outputs, cosine, sine, own = pl.pallas_call(
+        prepare_kernel,
+        out_shape=[*(pltpu.VMEM(a.shape, a.dtype) for a in caches), table, table, places],
+        in_specs=[smem()] * 3 + [vmem()] + [hbm()] * 3,
+        out_specs=[vmem()] * 6,
+        scratch_shapes=[pltpu.SemaphoreType.DMA((2 * batch_rows + 1,))],
+        compiler_params=pltpu.CompilerParams(vmem_limit_bytes=8 << 20),
+        name="prepare",
+    )(
+        later_index,
+        left(live_lengths),
+        left(owner_shard),
+        rates,
+        *(left(a) for a in caches),
+    )
     count = batch_rows * QUERY_GROUP
-    keys, values = pl.pallas_call(
-        load_kernel,
-        out_shape=[pltpu.VMEM(a.shape, a.dtype) for a in (key_cache_rows, value_cache_rows)],
-        in_specs=[hbm(), hbm()],
-        out_specs=[vmem(), vmem()],
-        scratch_shapes=[pltpu.SemaphoreType.DMA((2,))],
-        compiler_params=pltpu.CompilerParams(vmem_limit_bytes=8 << 20),
-        name="load",
-    )(left(key_cache_rows), left(value_cache_rows))
     message = pl.pallas_call(
         attend_kernel,
-        out_shape=pltpu.VMEM((shard_total, count + QUERY_GROUP, HEAD_SIZE), jnp.bfloat16),
-        in_specs=[smem(), smem()] + [vmem()] * 8,
+        out_shape=pltpu.VMEM((lax.axis_size(SEQ), count + QUERY_GROUP, HEAD_SIZE), jnp.bfloat16),
+        in_specs=[vmem()] * 9,
         out_specs=vmem(),
         scratch_shapes=[pltpu.VMEM((rows, HEAD_SIZE), jnp.float32)],
         compiler_params=pltpu.CompilerParams(vmem_limit_bytes=8 << 20),
         name="attend",
     )(
-        own_length,
-        is_owner,
-        *(held(a) for a in (parts, beside, around, across, cosine, sine, keys, values)),
+        *(held(a) for a in (parts, beside, around, across, cosine, sine, own, keys, values)),
     )
     got = lax.all_to_all(message, SEQ, 0, 0, tiled=True)
-    aux = got[:, count:, :count].astype(jnp.float32)
-    tops = aux[:, 0] + aux[:, 1] + aux[:, 2]
-    weights = jnp.exp(tops - jnp.max(tops, 0))
-    totals = jnp.sum(weights * (aux[:, 3] + aux[:, 4]), 0)
-    accum = jnp.sum(weights[..., None] * got[:, :count].astype(jnp.float32), 0)
-    attended = (accum / totals[..., None]).astype(jnp.bfloat16).reshape(batch_rows, QUERY_GROUP * HEAD_SIZE)
-    partial_value = jnp.dot(attended, output_weight, preferred_element_type=jnp.float32)
+    partial_value = pl.pallas_call(
+        merge_kernel,
+        out_shape=pltpu.VMEM((batch_rows, HEAD_SIZE), jnp.float32),
+        in_specs=[vmem()] * 2,
+        out_specs=vmem(),
+        compiler_params=pltpu.CompilerParams(vmem_limit_bytes=8 << 20),
+        name="merge",
+    )(held(got), held(outputs))
     other = lax.ppermute(partial_value, "kv", ((0, 1), (1, 0)))
     return (partial_value + other).astype(jnp.bfloat16)
 

time: 51.8 us -> 51.3 us (level)
  blocking collectives: 17.5 us -> 33.8 us
  starting transfers between devices: 15.9 us -> 8.4 us
  waiting for transfers between devices: 7.5 us -> 0.91 us
  other arithmetic: 3.54 us -> 0.67 us
  Pallas kernels: 6.44 us -> 7.17 us
    all_to_all x0 -> x1, blocking collectives: none -> 15.9 us  [local(): got = lax.all_to_all(copies, SEQ[1:], 0, 0, tiled=True)]
    all_to_all x1 -> x0, starting transfers between devices: 7.6 us -> none  [local(): parts = lax.all_to_all(copies, SEQ[1:], 0, 0, tiled=True).sum(0)]
    all_to_all x1 -> x0, waiting for transfers between devices: 6.11 us -> none  [local(): parts = lax.all_to_all(copies, SEQ[1:], 0, 0, tiled=True).sum(0)]
    pallas_call x2 -> x3, Pallas kernels: 4.54 us -> 6.02 us  [the longest x1 3 us: local(): pl.pallas_call(prepare_kernel, out_shape=[*(pltpu.VMEM(a.shape, a.dtype)...]
    convert_element_type x3 -> x0, other arithmetic: 1.35 us -> none  [the longest x1 0.67 us: local(): angles = position.astype(jnp.float32)[:, None] * frequencies()[None, :]]
    reduce_sum x4 -> x1, other arithmetic: 1.29 us -> 0.02 us  [local(): parts = got.sum(0)]
    pallas_call x1, Pallas kernels: 1.9 us -> 1.15 us  [local(): pl.pallas_call(project_kernel, out_shape=pltpu.VMEM((lax.axis_size(SEQ[1:...]
  transfers between devices with their start and end apart: 5 -> 4, of which waited for: 3 -> 2; matrix products, arithmetic and copies ran while one was open for 5% -> 0% of each run, Pallas kernels for 4% -> 6%
where the time goes in v3:
time: 51.3 us; the launch traced here: 51 us
  blocking collectives  33.8 us (66%)
  starting transfers between devices  8.4 us (16%)
  Pallas kernels  7.17 us (14%)
  waiting for transfers between devices  0.91 us (2%)
  other arithmetic  0.67 us (1%)
    all_to_all x1, blocking collectives, local(): got = lax.all_to_all(message, SEQ, 0, 0, tiled=True)  18 us
    all_to_all x1, blocking collectives, local(): got = lax.all_to_all(copies, SEQ[1:], 0, 0, tiled=True)  15.9 us
    ppermute x1, starting transfers between devices, local(): other = lax.ppermute(partial_value, 'kv', ((0, 1), (1, 0)))  3.99 us
    ppermute x1, starting transfers between devices, exchanges(): across = lax.ppermute(array, axis, ((0, 2), (2, 0), (1, 3), (3, 1)))  3.68 us
    pallas_call x1, Pallas kernels, local(): pl.pallas_call(prepare_kernel, out_shape=[*(pltpu.VMEM(a.shape, a.dtype)...  3 us
    pallas_call x1, Pallas kernels, local(): pl.pallas_call(attend_kernel, out_shape=pltpu.VMEM((lax.axis_size(SEQ), c...  2.04 us
    pallas_call x1, Pallas kernels, local(): pl.pallas_call(project_kernel, out_shape=pltpu.VMEM((lax.axis_size(SEQ[1:...  1.15 us
  transfers between devices with their start and end apart: 4, of which 2 were waited for; matrix products, arithmetic and copies ran while one was open for 0% of the time, Pallas kernels for 6%

profile of v3, /device:TPU:1, one launch (start us, length us, event | category | flops | bytes accessed | tf_op | source)
XLA Modules:
  0.0 51.0 jit_solution(13785304500100874098)
XLA Ops:
  0.0 0.1 maximum_bitcast_fusion.rate_ref
  0.1 1.2 %project.1 = f32[16,40,128]{2,1,0:T(8,128)S(1)} custom-call(s32[1]{0:T(128)} %bitcast.shard_ref, bf16[4,8192]{1,0:T(4,128)(2,1)} %state_ref.1, bf16[128,1024]{1,0:T(8,128)(2,1)} %query_ref.1, bf16[128,256]{1,0:T(8,128)(2,1)} %keyval_ref.1), custom_call_target="tpu_custom_call" | custom-call | tf_op jit(solution)/shard_map/project/pallas_call | solution.py:238
  1.3 15.9 %all_to_all.10 = f32[16,40,128]{2,1,0:T(8,128)S(1)} all-to-all(f32[16,40,128]{2,1,0:T(8,128)S(1)} %project.1), channel_id=1, replica_groups=mesh['kv'=2,'seq_0'=4,'seq_1'=4,'seq_2'=4,'dp'=1] {'seq_1','seq_2'}, dimensions={0} | all-to-all | bytes 655360 | tf_op jit(solution)/shard_map/all_to_all | solution.py:252
  17.1 3.7 %collective-permute-start.2 = (f32[40,128]{1,0:T(8,128)S(1)}, f32[40,128]{1,0:T(8,128)S(1)}, u32[]{:S(2)}, u32[]{:S(2)}) collective-permute-start(f32[40,128]{1,0:T(8,128)S(1)} %reduce_sum.9.part_ref), channel_id=1, source_target_pairs={{0,32},{32,0},{16,48},{48,16},{1,33},{33,1},{17,49},{49,17},{2,34}... | collective-permute-start | bytes 61448 | tf_op jit(solution)/shard_map/ppermute | solution.py:22
  20.8 0.4 collective-permute-start.1
  21.2 0.3 collective-permute-start
  21.6 3.0 %prepare.1 = (bf16[4,1,2048,128]{3,2,1,0:T(8,128)(2,1)S(1)}, bf16[4,1,2048,128]{3,2,1,0:T(8,128)(2,1)S(1)}, bf16[1024,128]{1,0:T(8,128)(2,1)S(1)}, f32[8,128]{1,...) custom-call(s32[1]{0:T(128)} %bitcast.shard_ref, s32[4,64]{1,0:T(4,128)} %live_ref.1, s32[4]{0:T(128)} %owner_ref.1, ...), custom_call_target="tpu_custom_call" | custom-call | tf_op jit(solution)/shard_map/prepare/pallas_call | solution.py:259
  24.6 0.0 collective-permute-done.2.across_ref
  24.6 0.1 collective-permute-done.1.around_ref
  24.7 0.0 collective-permute-done.beside_ref
  24.7 2.0 %attend.1 = bf16[64,40,128]{2,1,0:T(8,128)(2,1)S(1)} custom-call(f32[40,128]{1,0:T(8,128)S(1)} %reduce_sum.9.part_ref, f32[40,128]{1,0:T(8,128)S(1)} %collective-permute-done.beside_ref, f32[40,128]{1,0:T(8,128)S(1)} %collective-permute-done.1.around_ref, f32[40,128]{1,0:T(8,128)S(1)} %collective-permute-done.2.across_ref, ...), custom_call_target="tpu_custom_call" | custom-call | tf_op jit(solution)/shard_map/attend/pallas_call | solution.py:275
  26.7 18.0 %all_to_all.11.got_ref = bf16[64,40,128]{2,1,0:T(8,128)(2,1)S(1)} all-to-all(bf16[64,40,128]{2,1,0:T(8,128)(2,1)S(1)} %attend.1), channel_id=1, replica_groups=mesh['kv'=2,'seq_0'=4,'seq_1'=4,'seq_2'=4,'dp'=1] {'seq_0','seq_1','seq_2'}, dimensions={0} | all-to-all | bytes 1310720 | tf_op jit(solution)/shard_map/all_to_all | solution.py:286
  44.7 1.0 %merge.1 = f32[4,128]{1,0:T(4,128)S(1)} custom-call(bf16[64,40,128]{2,1,0:T(8,128)(2,1)S(1)} %all_to_all.11.got_ref, bf16[1024,128]{1,0:T(8,128)(2,1)S(1)} %get-tuple-element.26.output_ref), custom_call_target="tpu_custom_call" | custom-call | tf_op jit(solution)/shard_map/merge/pallas_call | solution.py:287
  45.7 4.0 %collective-permute-start.3 = (f32[4,128]{1,0:T(4,128)S(1)}, f32[4,128]{1,0:T(4,128)S(1)}, u32[]{:S(2)}, u32[]{:S(2)}) collective-permute-start(f32[4,128]{1,0:T(4,128)S(1)} %merge.1), channel_id=1, source_target_pairs={{0,64},{64,0},{1,65},{65,1},{2,66},{66,2},{3,67},{67,3},{4,68},{68... | collective-permute-start | bytes 6152 | tf_op jit(solution)/shard_map/ppermute | solution.py:295
  49.7 0.8 %collective-permute-done.3 = f32[4,128]{1,0:T(4,128)S(1)} collective-permute-done((f32[4,128]{1,0:T(4,128)S(1)}, f32[4,128]{1,0:T(4,128)S(1)}, u32[]{:S(2)}, u32[]{:S(2)}) %collective-permute-start.3) | collective-permute-done | bytes 2080 | tf_op jit(solution)/shard_map/ppermute | solution.py:295
  50.5 0.6 %add_convert_fusion = bf16[4,128]{1,0:T(4,128)(2,1)} fusion(f32[4,128]{1,0:T(4,128)S(1)} %merge.1, f32[4,128]{1,0:T(4,128)S(1)} %collective-permute-done.3), kind=kLoop, calls=%fused_computation | loop fusion | flops 1024 | bytes 5120 | tf_op jit(solution)/shard_map/convert_element_type | solution.py:296
  (2 shorter events, 0.0 us)
Async XLA Ops:
  17.1 7.4 %collective-permute-start.2 = (f32[40,128]{1,0:T(8,128)S(1)}, f32[40,128]{1,0:T(8,128)S(1)}, u32[]{:S(2)}, u32[]{:S(2)}) collective-permute-start(f32[40,128]{1,0:T(8,128)S(1)} %reduce_sum.9.part_ref), channel_id=1, source_target_pairs={{0,32},{32,0},{16,48},{48,16},{1,33},{33,1},{17,49},{49,17},{2,34}... | collective-permute-start | bytes 61448 | tf_op jit(solution)/shard_map/ppermute | solution.py:22
  20.8 3.8 %collective-permute-start.1 = (f32[40,128]{1,0:T(8,128)S(1)}, f32[40,128]{1,0:T(8,128)S(1)}, u32[]{:S(2)}, u32[]{:S(2)}) collective-permute-start(f32[40,128]{1,0:T(8,128)S(1)} %reduce_sum.9.part_ref), channel_id=1, source_target_pairs={{0,48},{48,0},{16,32},{32,16},{1,49},{49,1},{17,33},{33,17},{2,50}... | collective-permute-start | bytes 61448 | tf_op jit(solution)/shard_map/ppermute | solution.py:21
  21.2 3.4 %collective-permute-start = (f32[40,128]{1,0:T(8,128)S(1)}, f32[40,128]{1,0:T(8,128)S(1)}, u32[]{:S(2)}, u32[]{:S(2)}) collective-permute-start(f32[40,128]{1,0:T(8,128)S(1)} %reduce_sum.9.part_ref), channel_id=1, source_target_pairs={{0,16},{16,0},{32,48},{48,32},{1,17},{17,1},{33,49},{49,33},{2,18}... | collective-permute-start | bytes 61448 | tf_op jit(solution)/shard_map/ppermute | solution.py:20
  45.7 4.8 %collective-permute-start.3 = (f32[4,128]{1,0:T(4,128)S(1)}, f32[4,128]{1,0:T(4,128)S(1)}, u32[]{:S(2)}, u32[]{:S(2)}) collective-permute-start(f32[4,128]{1,0:T(4,128)S(1)} %merge.1), channel_id=1, source_target_pairs={{0,64},{64,0},{1,65},{65,1},{2,66},{66,2},{3,67},{67,3},{4,68},{68... | collective-permute-start | bytes 6152 | tf_op jit(solution)/shard_map/ppermute | solution.py:295

commit v4 on v3

--- a/solution.py
+++ b/solution.py
@@ -120,26 +120,29 @@
         value_new = turned[batch + b : batch + b + 1].astype(jnp.bfloat16)
         picks.append((query, key_new.astype(jnp.float32), value_new.astype(jnp.float32)))
     slot = lax.broadcasted_iota(jnp.int32, (QUERY_GROUP, slots), 1)
-    accums = []
+    scores_of = [
+        lax.dot_general(query, key_ref[b, 0], (((1,), (1,)), ((), ())), preferred_element_type=jnp.float32)
+        * scaling
+        for b, (query, _, _) in enumerate(picks)
+    ]
+    probs, additions = [], []
     for b, (query, key_new, value_new) in enumerate(picks):
-        scores = (
-            lax.dot_general(
-                query, key_ref[b, 0], (((1,), (1,)), ((), ())), preferred_element_type=jnp.float32
-            )
-            * scaling
-        )
-        scores = jnp.where(slot < own_ref[b : b + 1, 0:1], scores, -jnp.inf)
+        scores = jnp.where(slot < own_ref[b : b + 1, 0:1], scores_of[b], -jnp.inf)
         new_score = jnp.sum(query.astype(jnp.float32) * key_new, -1, keepdims=True) * scaling
         owns = own_ref[batch + b : batch + b + 1, 0:1] > 0
         top = jnp.maximum(jnp.max(scores, -1, keepdims=True), jnp.where(owns, new_score, -jnp.inf))
         prob = jnp.exp(scores - top).astype(jnp.bfloat16)
         new_prob = jnp.where(owns, jnp.exp(new_score - top), 0.0).astype(jnp.bfloat16).astype(jnp.float32)
         weight = jnp.sum(prob.astype(jnp.float32), -1, keepdims=True) + new_prob
-        accum = jnp.dot(prob, value_ref[b, 0], preferred_element_type=jnp.float32) + new_prob * value_new
-        accums.append(accum)
+        probs.append(prob)
+        additions.append(new_prob * value_new)
         mine = lane == sublane + b * QUERY_GROUP
         top_row += jnp.sum(jnp.where(mine, top, 0.0), 0, keepdims=True)
         total_row += jnp.sum(jnp.where(mine, weight, 0.0), 0, keepdims=True)
+    accums = [
+        jnp.dot(prob, value_ref[b, 0], preferred_element_type=jnp.float32) + additions[b]
+        for b, prob in enumerate(probs)
+    ]
     side = jnp.zeros((QUERY_GROUP, HEAD_SIZE), jnp.float32)
     at = 0
     for row, count in ((top_row, 3), (total_row, 2)):
@@ -158,18 +161,16 @@
     batch = out_ref.shape[0]
     count = batch * QUERY_GROUP
     side = got_ref[:, count:, :].astype(jnp.float32).reshape(sources * QUERY_GROUP, HEAD_SIZE).astype(jnp.bfloat16)
-    source = lax.broadcasted_iota(jnp.int32, (HEAD_SIZE, sources * QUERY_GROUP), 0)
-    entry = lax.broadcasted_iota(jnp.int32, (HEAD_SIZE, sources * QUERY_GROUP), 1)
+    source = lax.broadcasted_iota(jnp.int32, (2 * sources, sources * QUERY_GROUP), 0)
+    entry = lax.broadcasted_iota(jnp.int32, (2 * sources, sources * QUERY_GROUP), 1)
     place = entry - source * QUERY_GROUP
-
-    def gathered(low, high):
-        chosen = ((place >= low) & (place < high)).astype(jnp.float32).astype(jnp.bfloat16)
-        return jnp.dot(chosen, side, preferred_element_type=jnp.float32).T[:count]
-
-    there = lax.broadcasted_iota(jnp.int32, (count, HEAD_SIZE), 1) < sources
-    tops = jnp.where(there, gathered(0, 3), -jnp.inf)
+    of_total = place + sources * QUERY_GROUP
+    chosen = ((place >= 0) & (place < 3)) | ((of_total >= 3) & (of_total < 5))
+    chosen = chosen.astype(jnp.float32).astype(jnp.bfloat16)
+    found = jnp.dot(chosen, side, preferred_element_type=jnp.float32).T[:count]
+    tops, totals = found[:, :sources], found[:, sources:]
     weights = jnp.exp(tops - jnp.max(tops, -1, keepdims=True))
-    total = jnp.sum(weights * gathered(3, 5), -1, keepdims=True)
+    total = jnp.sum(weights * totals, -1, keepdims=True)
     accum = jnp.zeros((count, HEAD_SIZE), jnp.float32)
     for at in range(sources):
         accum += weights[:, at : at + 1] * got_ref[at, :count, :].astype(jnp.float32)

time: 51.3 us -> 50.3 us (0.981)
  Pallas kernels: 7.17 us -> 6.2 us
    pallas_call x1, Pallas kernels: 2.04 us -> 1.07 us  [local(): pl.pallas_call(attend_kernel, out_shape=pltpu.VMEM((lax.axis_size(SEQ), c...]
where the time goes in v4:
time: 50.3 us; the launch traced here: 50.1 us
  blocking collectives  33.8 us (67%)
  starting transfers between devices  8.4 us (17%)
  Pallas kernels  6.2 us (12%)
  waiting for transfers between devices  0.91 us (2%)
  other arithmetic  0.67 us (1%)
    all_to_all x1, blocking collectives, local(): got = lax.all_to_all(message, SEQ, 0, 0, tiled=True)  18 us
    all_to_all x1, blocking collectives, local(): got = lax.all_to_all(copies, SEQ[1:], 0, 0, tiled=True)  15.9 us
    ppermute x1, starting transfers between devices, local(): other = lax.ppermute(partial_value, 'kv', ((0, 1), (1, 0)))  3.99 us
    ppermute x1, starting transfers between devices, exchanges(): across = lax.ppermute(array, axis, ((0, 2), (2, 0), (1, 3), (3, 1)))  3.68 us
    pallas_call x1, Pallas kernels, local(): pl.pallas_call(prepare_kernel, out_shape=[*(pltpu.VMEM(a.shape, a.dtype)...  3 us
    pallas_call x1, Pallas kernels, local(): pl.pallas_call(project_kernel, out_shape=pltpu.VMEM((lax.axis_size(SEQ[1:...  1.15 us
    pallas_call x1, Pallas kernels, local(): pl.pallas_call(attend_kernel, out_shape=pltpu.VMEM((lax.axis_size(SEQ), c...  1.07 us
  transfers between devices with their start and end apart: 4, of which 2 were waited for; matrix products, arithmetic and copies ran while one was open for 0% of the time, Pallas kernels for 6%

profile of v4, /device:TPU:1, one launch (start us, length us, event | category | flops | bytes accessed | tf_op | source)
XLA Modules:
  0.0 50.1 jit_solution(3966399612141784511)
XLA Ops:
  0.0 0.1 maximum_bitcast_fusion.rate_ref
  0.1 1.2 %project.1 = f32[16,40,128]{2,1,0:T(8,128)S(1)} custom-call(s32[1]{0:T(128)} %bitcast.shard_ref, bf16[4,8192]{1,0:T(4,128)(2,1)} %state_ref.1, bf16[128,1024]{1,0:T(8,128)(2,1)} %query_ref.1, bf16[128,256]{1,0:T(8,128)(2,1)} %keyval_ref.1), custom_call_target="tpu_custom_call" | custom-call | tf_op jit(solution)/shard_map/project/pallas_call | solution.py:239
  1.3 15.9 %all_to_all.10 = f32[16,40,128]{2,1,0:T(8,128)S(1)} all-to-all(f32[16,40,128]{2,1,0:T(8,128)S(1)} %project.1), channel_id=1, replica_groups=mesh['kv'=2,'seq_0'=4,'seq_1'=4,'seq_2'=4,'dp'=1] {'seq_1','seq_2'}, dimensions={0} | all-to-all | bytes 655360 | tf_op jit(solution)/shard_map/all_to_all | solution.py:253
  17.1 3.7 %collective-permute-start.2 = (f32[40,128]{1,0:T(8,128)S(1)}, f32[40,128]{1,0:T(8,128)S(1)}, u32[]{:S(2)}, u32[]{:S(2)}) collective-permute-start(f32[40,128]{1,0:T(8,128)S(1)} %reduce_sum.9.part_ref), channel_id=1, source_target_pairs={{0,32},{32,0},{16,48},{48,16},{1,33},{33,1},{17,49},{49,17},{2,34}... | collective-permute-start | bytes 61448 | tf_op jit(solution)/shard_map/ppermute | solution.py:22
  20.8 0.4 collective-permute-start.1
  21.2 0.3 collective-permute-start
  21.6 3.0 %prepare.1 = (bf16[4,1,2048,128]{3,2,1,0:T(8,128)(2,1)S(1)}, bf16[4,1,2048,128]{3,2,1,0:T(8,128)(2,1)S(1)}, bf16[1024,128]{1,0:T(8,128)(2,1)S(1)}, f32[8,128]{1,...) custom-call(s32[1]{0:T(128)} %bitcast.shard_ref, s32[4,64]{1,0:T(4,128)} %live_ref.1, s32[4]{0:T(128)} %owner_ref.1, ...), custom_call_target="tpu_custom_call" | custom-call | tf_op jit(solution)/shard_map/prepare/pallas_call | solution.py:260
  24.6 0.0 collective-permute-done.2.across_ref
  24.6 0.1 collective-permute-done.1.around_ref
  24.7 0.0 collective-permute-done.beside_ref
  24.7 1.1 %attend.1 = bf16[64,40,128]{2,1,0:T(8,128)(2,1)S(1)} custom-call(f32[40,128]{1,0:T(8,128)S(1)} %reduce_sum.9.part_ref, f32[40,128]{1,0:T(8,128)S(1)} %collective-permute-done.beside_ref, f32[40,128]{1,0:T(8,128)S(1)} %collective-permute-done.1.around_ref, f32[40,128]{1,0:T(8,128)S(1)} %collective-permute-done.2.across_ref, ...), custom_call_target="tpu_custom_call" | custom-call | tf_op jit(solution)/shard_map/attend/pallas_call | solution.py:276
  25.7 18.0 %all_to_all.11.got_ref = bf16[64,40,128]{2,1,0:T(8,128)(2,1)S(1)} all-to-all(bf16[64,40,128]{2,1,0:T(8,128)(2,1)S(1)} %attend.1), channel_id=1, replica_groups=mesh['kv'=2,'seq_0'=4,'seq_1'=4,'seq_2'=4,'dp'=1] {'seq_0','seq_1','seq_2'}, dimensions={0} | all-to-all | bytes 1310720 | tf_op jit(solution)/shard_map/all_to_all | solution.py:287
  43.7 1.0 %merge.1 = f32[4,128]{1,0:T(4,128)S(1)} custom-call(bf16[64,40,128]{2,1,0:T(8,128)(2,1)S(1)} %all_to_all.11.got_ref, bf16[1024,128]{1,0:T(8,128)(2,1)S(1)} %get-tuple-element.26.output_ref), custom_call_target="tpu_custom_call" | custom-call | tf_op jit(solution)/shard_map/merge/pallas_call | solution.py:288
  44.7 4.0 %collective-permute-start.3 = (f32[4,128]{1,0:T(4,128)S(1)}, f32[4,128]{1,0:T(4,128)S(1)}, u32[]{:S(2)}, u32[]{:S(2)}) collective-permute-start(f32[4,128]{1,0:T(4,128)S(1)} %merge.1), channel_id=1, source_target_pairs={{0,64},{64,0},{1,65},{65,1},{2,66},{66,2},{3,67},{67,3},{4,68},{68... | collective-permute-start | bytes 6152 | tf_op jit(solution)/shard_map/ppermute | solution.py:296
  48.7 0.8 %collective-permute-done.3 = f32[4,128]{1,0:T(4,128)S(1)} collective-permute-done((f32[4,128]{1,0:T(4,128)S(1)}, f32[4,128]{1,0:T(4,128)S(1)}, u32[]{:S(2)}, u32[]{:S(2)}) %collective-permute-start.3) | collective-permute-done | bytes 2080 | tf_op jit(solution)/shard_map/ppermute | solution.py:296
  49.5 0.6 %add_convert_fusion = bf16[4,128]{1,0:T(4,128)(2,1)} fusion(f32[4,128]{1,0:T(4,128)S(1)} %merge.1, f32[4,128]{1,0:T(4,128)S(1)} %collective-permute-done.3), kind=kLoop, calls=%fused_computation | loop fusion | flops 1024 | bytes 5120 | tf_op jit(solution)/shard_map/convert_element_type | solution.py:297
  (2 shorter events, 0.0 us)
Async XLA Ops:
  17.1 7.4 %collective-permute-start.2 = (f32[40,128]{1,0:T(8,128)S(1)}, f32[40,128]{1,0:T(8,128)S(1)}, u32[]{:S(2)}, u32[]{:S(2)}) collective-permute-start(f32[40,128]{1,0:T(8,128)S(1)} %reduce_sum.9.part_ref), channel_id=1, source_target_pairs={{0,32},{32,0},{16,48},{48,16},{1,33},{33,1},{17,49},{49,17},{2,34}... | collective-permute-start | bytes 61448 | tf_op jit(solution)/shard_map/ppermute | solution.py:22
  20.8 3.8 %collective-permute-start.1 = (f32[40,128]{1,0:T(8,128)S(1)}, f32[40,128]{1,0:T(8,128)S(1)}, u32[]{:S(2)}, u32[]{:S(2)}) collective-permute-start(f32[40,128]{1,0:T(8,128)S(1)} %reduce_sum.9.part_ref), channel_id=1, source_target_pairs={{0,48},{48,0},{16,32},{32,16},{1,49},{49,1},{17,33},{33,17},{2,50}... | collective-permute-start | bytes 61448 | tf_op jit(solution)/shard_map/ppermute | solution.py:21
  21.2 3.4 %collective-permute-start = (f32[40,128]{1,0:T(8,128)S(1)}, f32[40,128]{1,0:T(8,128)S(1)}, u32[]{:S(2)}, u32[]{:S(2)}) collective-permute-start(f32[40,128]{1,0:T(8,128)S(1)} %reduce_sum.9.part_ref), channel_id=1, source_target_pairs={{0,16},{16,0},{32,48},{48,32},{1,17},{17,1},{33,49},{49,33},{2,18}... | collective-permute-start | bytes 61448 | tf_op jit(solution)/shard_map/ppermute | solution.py:20
  44.7 4.8 %collective-permute-start.3 = (f32[4,128]{1,0:T(4,128)S(1)}, f32[4,128]{1,0:T(4,128)S(1)}, u32[]{:S(2)}, u32[]{:S(2)}) collective-permute-start(f32[4,128]{1,0:T(4,128)S(1)} %merge.1), channel_id=1, source_target_pairs={{0,64},{64,0},{1,65},{65,1},{2,66},{66,2},{3,67},{67,3},{4,68},{68... | collective-permute-start | bytes 6152 | tf_op jit(solution)/shard_map/ppermute | solution.py:296

commit v5 on v4

--- a/solution.py
+++ b/solution.py
@@ -17,8 +17,8 @@
 
 
 def exchanges(array, axis):
-    beside = lax.ppermute(array, axis, ((0, 1), (1, 0), (2, 3), (3, 2)))
-    around = lax.ppermute(array, axis, ((0, 3), (3, 0), (1, 2), (2, 1)))
+    beside = lax.ppermute(array, axis, ((0, 1), (1, 2), (2, 3), (3, 0)))
+    around = lax.ppermute(array, axis, ((0, 3), (1, 0), (2, 1), (3, 2)))
     across = lax.ppermute(array, axis, ((0, 2), (2, 0), (1, 3), (3, 1)))
     return beside, around, across
 
@@ -102,7 +102,7 @@
     straight = lax.broadcasted_iota(jnp.int32, cosine.shape, 0) >= batch
     for at in range(0, score_ref.shape[0], 2 * batch):
         tile = pl.ds(at, 2 * batch)
-        total = (part_ref[tile, :] + beside_ref[tile, :]) + (around_ref[tile, :] + across_ref[tile, :])
+        total = (part_ref[tile, :] + across_ref[tile, :]) + (beside_ref[tile, :] + around_ref[tile, :])
         if at + 2 * batch == score_ref.shape[0]:
             cosine = jnp.where(straight, 1.0, cosine)
             sine = jnp.where(straight, 0.0, sine)

time: 50.3 us -> 49.6 us (0.986)
  blocking collectives: 33.8 us -> 32.4 us
  starting transfers between devices: 8.4 us -> 9.12 us
    all_to_all x1, blocking collectives: 18 us -> 16.6 us  [local(): got = lax.all_to_all(message, SEQ, 0, 0, tiled=True)]
    ppermute x2, starting transfers between devices: 0.74 us -> 1.47 us  [the longest x1 1.03 us: exchanges(): beside = lax.ppermute(array, axis, ((0, 1), (1, 2), (2, 3), (3, 0)))]
  transfers between devices with their start and end apart: 4 -> 4, of which waited for: 2 -> 1; matrix products, arithmetic and copies ran while one was open for 0% -> 0% of each run, Pallas kernels for 6% -> 6%
where the time goes in v5:
time: 49.6 us; the launch traced here: 49.3 us
  blocking collectives  32.4 us (65%)
  starting transfers between devices  9.12 us (18%)
  Pallas kernels  6.21 us (13%)
  waiting for transfers between devices  0.83 us (2%)
  other arithmetic  0.67 us (1%)
    all_to_all x1, blocking collectives, local(): got = lax.all_to_all(message, SEQ, 0, 0, tiled=True)  16.6 us
    all_to_all x1, blocking collectives, local(): got = lax.all_to_all(copies, SEQ[1:], 0, 0, tiled=True)  15.9 us
    ppermute x1, starting transfers between devices, local(): other = lax.ppermute(partial_value, 'kv', ((0, 1), (1, 0)))  3.98 us
    ppermute x1, starting transfers between devices, exchanges(): across = lax.ppermute(array, axis, ((0, 2), (2, 0), (1, 3), (3, 1)))  3.68 us
    pallas_call x1, Pallas kernels, local(): pl.pallas_call(prepare_kernel, out_shape=[*(pltpu.VMEM(a.shape, a.dtype)...  3 us
    pallas_call x1, Pallas kernels, local(): pl.pallas_call(project_kernel, out_shape=pltpu.VMEM((lax.axis_size(SEQ[1:...  1.15 us
    pallas_call x1, Pallas kernels, local(): pl.pallas_call(attend_kernel, out_shape=pltpu.VMEM((lax.axis_size(SEQ), c...  1.07 us
    ppermute x1, starting transfers between devices, exchanges(): beside = lax.ppermute(array, axis, ((0, 1), (1, 2), (2, 3), (3, 0)))  1.03 us
  transfers between devices with their start and end apart: 4, of which 1 were waited for; matrix products, arithmetic and copies ran while one was open for 0% of the time, Pallas kernels for 6%

profile of v5, /device:TPU:1, one launch (start us, length us, event | category | flops | bytes accessed | tf_op | source)
XLA Modules:
  0.0 49.3 jit_solution(6508626164802835416)
XLA Ops:
  0.0 0.1 maximum_bitcast_fusion.rate_ref
  0.1 1.2 %project.1 = f32[16,40,128]{2,1,0:T(8,128)S(1)} custom-call(s32[1]{0:T(128)} %bitcast.shard_ref, bf16[4,8192]{1,0:T(4,128)(2,1)} %state_ref.1, bf16[128,1024]{1,0:T(8,128)(2,1)} %query_ref.1, bf16[128,256]{1,0:T(8,128)(2,1)} %keyval_ref.1), custom_call_target="tpu_custom_call" | custom-call | tf_op jit(solution)/shard_map/project/pallas_call | solution.py:239
  1.3 15.9 %all_to_all.10 = f32[16,40,128]{2,1,0:T(8,128)S(1)} all-to-all(f32[16,40,128]{2,1,0:T(8,128)S(1)} %project.1), channel_id=1, replica_groups=mesh['kv'=2,'seq_0'=4,'seq_1'=4,'seq_2'=4,'dp'=1] {'seq_1','seq_2'}, dimensions={0} | all-to-all | bytes 655360 | tf_op jit(solution)/shard_map/all_to_all | solution.py:253
  17.1 3.7 %collective-permute-start.2 = (f32[40,128]{1,0:T(8,128)S(1)}, f32[40,128]{1,0:T(8,128)S(1)}, u32[]{:S(2)}, u32[]{:S(2)}) collective-permute-start(f32[40,128]{1,0:T(8,128)S(1)} %reduce_sum.9.part_ref), channel_id=1, source_target_pairs={{0,32},{32,0},{16,48},{48,16},{1,33},{33,1},{17,49},{49,17},{2,34}... | collective-permute-start | bytes 61448 | tf_op jit(solution)/shard_map/ppermute | solution.py:22
  20.8 0.4 collective-permute-start.1
  21.2 1.0 %collective-permute-start = (f32[40,128]{1,0:T(8,128)S(1)}, f32[40,128]{1,0:T(8,128)S(1)}, u32[]{:S(2)}, u32[]{:S(2)}) collective-permute-start(f32[40,128]{1,0:T(8,128)S(1)} %reduce_sum.9.part_ref), channel_id=1, source_target_pairs={{0,16},{16,32},{32,48},{48,0},{1,17},{17,33},{33,49},{49,1},{2,18}... | collective-permute-start | bytes 61448 | tf_op jit(solution)/shard_map/ppermute | solution.py:20
  22.3 3.0 %prepare.1 = (bf16[4,1,2048,128]{3,2,1,0:T(8,128)(2,1)S(1)}, bf16[4,1,2048,128]{3,2,1,0:T(8,128)(2,1)S(1)}, bf16[1024,128]{1,0:T(8,128)(2,1)S(1)}, f32[8,128]{1,...) custom-call(s32[1]{0:T(128)} %bitcast.shard_ref, s32[4,64]{1,0:T(4,128)} %live_ref.1, s32[4]{0:T(128)} %owner_ref.1, ...), custom_call_target="tpu_custom_call" | custom-call | tf_op jit(solution)/shard_map/prepare/pallas_call | solution.py:260
  25.3 0.0 collective-permute-done.2.across_ref
  25.3 0.0 collective-permute-done.1.around_ref
  25.3 0.0 collective-permute-done.beside_ref
  25.3 1.1 %attend.1 = bf16[64,40,128]{2,1,0:T(8,128)(2,1)S(1)} custom-call(f32[40,128]{1,0:T(8,128)S(1)} %reduce_sum.9.part_ref, f32[40,128]{1,0:T(8,128)S(1)} %collective-permute-done.beside_ref, f32[40,128]{1,0:T(8,128)S(1)} %collective-permute-done.1.around_ref, f32[40,128]{1,0:T(8,128)S(1)} %collective-permute-done.2.across_ref, ...), custom_call_target="tpu_custom_call" | custom-call | tf_op jit(solution)/shard_map/attend/pallas_call | solution.py:276
  26.4 16.6 %all_to_all.11.got_ref = bf16[64,40,128]{2,1,0:T(8,128)(2,1)S(1)} all-to-all(bf16[64,40,128]{2,1,0:T(8,128)(2,1)S(1)} %attend.1), channel_id=1, replica_groups=mesh['kv'=2,'seq_0'=4,'seq_1'=4,'seq_2'=4,'dp'=1] {'seq_0','seq_1','seq_2'}, dimensions={0} | all-to-all | bytes 1310720 | tf_op jit(solution)/shard_map/all_to_all | solution.py:287
  43.0 1.0 %merge.1 = f32[4,128]{1,0:T(4,128)S(1)} custom-call(bf16[64,40,128]{2,1,0:T(8,128)(2,1)S(1)} %all_to_all.11.got_ref, bf16[1024,128]{1,0:T(8,128)(2,1)S(1)} %get-tuple-element.26.output_ref), custom_call_target="tpu_custom_call" | custom-call | tf_op jit(solution)/shard_map/merge/pallas_call | solution.py:288
  44.0 4.0 %collective-permute-start.3 = (f32[4,128]{1,0:T(4,128)S(1)}, f32[4,128]{1,0:T(4,128)S(1)}, u32[]{:S(2)}, u32[]{:S(2)}) collective-permute-start(f32[4,128]{1,0:T(4,128)S(1)} %merge.1), channel_id=1, source_target_pairs={{0,64},{64,0},{1,65},{65,1},{2,66},{66,2},{3,67},{67,3},{4,68},{68... | collective-permute-start | bytes 6152 | tf_op jit(solution)/shard_map/ppermute | solution.py:296
  47.9 0.8 %collective-permute-done.3 = f32[4,128]{1,0:T(4,128)S(1)} collective-permute-done((f32[4,128]{1,0:T(4,128)S(1)}, f32[4,128]{1,0:T(4,128)S(1)}, u32[]{:S(2)}, u32[]{:S(2)}) %collective-permute-start.3) | collective-permute-done | bytes 2080 | tf_op jit(solution)/shard_map/ppermute | solution.py:296
  48.8 0.6 %add_convert_fusion = bf16[4,128]{1,0:T(4,128)(2,1)} fusion(f32[4,128]{1,0:T(4,128)S(1)} %merge.1, f32[4,128]{1,0:T(4,128)S(1)} %collective-permute-done.3), kind=kLoop, calls=%fused_computation | loop fusion | flops 1024 | bytes 5120 | tf_op jit(solution)/shard_map/convert_element_type | solution.py:297
  (2 shorter events, 0.0 us)
Async XLA Ops:
  17.1 8.2 %collective-permute-start.2 = (f32[40,128]{1,0:T(8,128)S(1)}, f32[40,128]{1,0:T(8,128)S(1)}, u32[]{:S(2)}, u32[]{:S(2)}) collective-permute-start(f32[40,128]{1,0:T(8,128)S(1)} %reduce_sum.9.part_ref), channel_id=1, source_target_pairs={{0,32},{32,0},{16,48},{48,16},{1,33},{33,1},{17,49},{49,17},{2,34}... | collective-permute-start | bytes 61448 | tf_op jit(solution)/shard_map/ppermute | solution.py:22
  20.8 4.5 %collective-permute-start.1 = (f32[40,128]{1,0:T(8,128)S(1)}, f32[40,128]{1,0:T(8,128)S(1)}, u32[]{:S(2)}, u32[]{:S(2)}) collective-permute-start(f32[40,128]{1,0:T(8,128)S(1)} %reduce_sum.9.part_ref), channel_id=1, source_target_pairs={{0,48},{16,0},{32,16},{48,32},{1,49},{17,1},{33,17},{49,33},{2,50}... | collective-permute-start | bytes 61448 | tf_op jit(solution)/shard_map/ppermute | solution.py:21
  21.2 4.1 %collective-permute-start = (f32[40,128]{1,0:T(8,128)S(1)}, f32[40,128]{1,0:T(8,128)S(1)}, u32[]{:S(2)}, u32[]{:S(2)}) collective-permute-start(f32[40,128]{1,0:T(8,128)S(1)} %reduce_sum.9.part_ref), channel_id=1, source_target_pairs={{0,16},{16,32},{32,48},{48,0},{1,17},{17,33},{33,49},{49,1},{2,18}... | collective-permute-start | bytes 61448 | tf_op jit(solution)/shard_map/ppermute | solution.py:20
  44.0 4.8 %collective-permute-start.3 = (f32[4,128]{1,0:T(4,128)S(1)}, f32[4,128]{1,0:T(4,128)S(1)}, u32[]{:S(2)}, u32[]{:S(2)}) collective-permute-start(f32[4,128]{1,0:T(4,128)S(1)} %merge.1), channel_id=1, source_target_pairs={{0,64},{64,0},{1,65},{65,1},{2,66},{66,2},{3,67},{67,3},{4,68},{68... | collective-permute-start | bytes 6152 | tf_op jit(solution)/shard_map/ppermute | solution.py:296

commit v6 on v5

--- a/solution.py
+++ b/solution.py
@@ -11,6 +11,12 @@
 HEAD_SIZE = 128
 QUERY_GROUP = 8
 SEQ = ("seq_0", "seq_1", "seq_2")
+MIXED = (
+    29, 28, 24, 33, 35, 60, 23, 40, 11, 27, 61, 3, 5, 7, 42, 45,
+    12, 59, 0, 55, 1, 44, 41, 14, 15, 17, 47, 20, 63, 10, 62, 54,
+    36, 51, 21, 4, 43, 52, 9, 38, 34, 58, 39, 6, 46, 18, 8, 57,
+    13, 37, 22, 30, 19, 53, 50, 25, 31, 32, 16, 2, 26, 56, 48, 49,
+)
 
 
 rope_theta = 500000.0
@@ -284,7 +290,7 @@
     )(
         *(held(a) for a in (parts, beside, around, across, cosine, sine, own, keys, values)),
     )
-    got = lax.all_to_all(message, SEQ, 0, 0, tiled=True)
+    got = lax.all_to_all(message, SEQ, 0, 0, tiled=True, axis_index_groups=[list(MIXED)])
     partial_value = pl.pallas_call(
         merge_kernel,
         out_shape=pltpu.VMEM((batch_rows, HEAD_SIZE), jnp.float32),

time: 49.6 us -> 48.2 us (0.972)
  blocking collectives: 32.4 us -> 31.4 us
    all_to_all x1, blocking collectives: 16.6 us -> 15.6 us  [local(): lax.all_to_all(message, SEQ, 0, 0, tiled=True, axis_index_groups=[list(MI...]
where the time goes in v6:
time: 48.2 us; the launch traced here: 48 us
  blocking collectives  31.4 us (65%)
  starting transfers between devices  8.78 us (18%)
  Pallas kernels  6.21 us (13%)
  waiting for transfers between devices  0.83 us (2%)
  other arithmetic  0.67 us (1%)
    all_to_all x1, blocking collectives, local(): got = lax.all_to_all(copies, SEQ[1:], 0, 0, tiled=True)  15.9 us
    all_to_all x1, blocking collectives, local(): lax.all_to_all(message, SEQ, 0, 0, tiled=True, axis_index_groups=[list(MI...  15.6 us
    ppermute x1, starting transfers between devices, exchanges(): across = lax.ppermute(array, axis, ((0, 2), (2, 0), (1, 3), (3, 1)))  3.68 us
    ppermute x1, starting transfers between devices, local(): other = lax.ppermute(partial_value, 'kv', ((0, 1), (1, 0)))  3.64 us
    pallas_call x1, Pallas kernels, local(): pl.pallas_call(prepare_kernel, out_shape=[*(pltpu.VMEM(a.shape, a.dtype)...  3 us
    pallas_call x1, Pallas kernels, local(): pl.pallas_call(project_kernel, out_shape=pltpu.VMEM((lax.axis_size(SEQ[1:...  1.15 us
    pallas_call x1, Pallas kernels, local(): pl.pallas_call(attend_kernel, out_shape=pltpu.VMEM((lax.axis_size(SEQ), c...  1.07 us
    ppermute x1, starting transfers between devices, exchanges(): beside = lax.ppermute(array, axis, ((0, 1), (1, 2), (2, 3), (3, 0)))  1.03 us
  transfers between devices with their start and end apart: 4, of which 1 were waited for; matrix products, arithmetic and copies ran while one was open for 0% of the time, Pallas kernels for 6%

profile of v6, /device:TPU:1, one launch (start us, length us, event | category | flops | bytes accessed | tf_op | source)
XLA Modules:
  0.0 48.0 jit_solution(17200791126298197709)
XLA Ops:
  0.0 0.1 maximum_bitcast_fusion.rate_ref
  0.1 1.2 %project.1 = f32[16,40,128]{2,1,0:T(8,128)S(1)} custom-call(s32[1]{0:T(128)} %bitcast.shard_ref, bf16[4,8192]{1,0:T(4,128)(2,1)} %state_ref.1, bf16[128,1024]{1,0:T(8,128)(2,1)} %query_ref.1, bf16[128,256]{1,0:T(8,128)(2,1)} %keyval_ref.1), custom_call_target="tpu_custom_call" | custom-call | tf_op jit(solution)/shard_map/project/pallas_call | solution.py:245
  1.3 15.9 %all_to_all.10 = f32[16,40,128]{2,1,0:T(8,128)S(1)} all-to-all(f32[16,40,128]{2,1,0:T(8,128)S(1)} %project.1), channel_id=1, replica_groups=mesh['kv'=2,'seq_0'=4,'seq_1'=4,'seq_2'=4,'dp'=1] {'seq_1','seq_2'}, dimensions={0} | all-to-all | bytes 655360 | tf_op jit(solution)/shard_map/all_to_all | solution.py:259
  17.1 3.7 %collective-permute-start.2 = (f32[40,128]{1,0:T(8,128)S(1)}, f32[40,128]{1,0:T(8,128)S(1)}, u32[]{:S(2)}, u32[]{:S(2)}) collective-permute-start(f32[40,128]{1,0:T(8,128)S(1)} %reduce_sum.9.part_ref), channel_id=1, source_target_pairs={{0,32},{32,0},{16,48},{48,16},{1,33},{33,1},{17,49},{49,17},{2,34}... | collective-permute-start | bytes 61448 | tf_op jit(solution)/shard_map/ppermute | solution.py:28
  20.8 0.4 collective-permute-start.1
  21.2 1.0 %collective-permute-start = (f32[40,128]{1,0:T(8,128)S(1)}, f32[40,128]{1,0:T(8,128)S(1)}, u32[]{:S(2)}, u32[]{:S(2)}) collective-permute-start(f32[40,128]{1,0:T(8,128)S(1)} %reduce_sum.9.part_ref), channel_id=1, source_target_pairs={{0,16},{16,32},{32,48},{48,0},{1,17},{17,33},{33,49},{49,1},{2,18}... | collective-permute-start | bytes 61448 | tf_op jit(solution)/shard_map/ppermute | solution.py:26
  22.3 3.0 %prepare.1 = (bf16[4,1,2048,128]{3,2,1,0:T(8,128)(2,1)S(1)}, bf16[4,1,2048,128]{3,2,1,0:T(8,128)(2,1)S(1)}, bf16[1024,128]{1,0:T(8,128)(2,1)S(1)}, f32[8,128]{1,...) custom-call(s32[1]{0:T(128)} %bitcast.shard_ref, s32[4,64]{1,0:T(4,128)} %live_ref.1, s32[4]{0:T(128)} %owner_ref.1, ...), custom_call_target="tpu_custom_call" | custom-call | tf_op jit(solution)/shard_map/prepare/pallas_call | solution.py:266
  25.3 0.0 collective-permute-done.2.across_ref
  25.3 0.0 collective-permute-done.1.around_ref
  25.3 0.0 collective-permute-done.beside_ref
  25.3 1.1 %attend.1 = bf16[64,40,128]{2,1,0:T(8,128)(2,1)S(1)} custom-call(f32[40,128]{1,0:T(8,128)S(1)} %reduce_sum.9.part_ref, f32[40,128]{1,0:T(8,128)S(1)} %collective-permute-done.beside_ref, f32[40,128]{1,0:T(8,128)S(1)} %collective-permute-done.1.around_ref, f32[40,128]{1,0:T(8,128)S(1)} %collective-permute-done.2.across_ref, ...), custom_call_target="tpu_custom_call" | custom-call | tf_op jit(solution)/shard_map/attend/pallas_call | solution.py:282
  26.4 15.6 %all_to_all.11.got_ref = bf16[64,40,128]{2,1,0:T(8,128)(2,1)S(1)} all-to-all(bf16[64,40,128]{2,1,0:T(8,128)(2,1)S(1)} %attend.1), channel_id=1, replica_groups={{29,28,24,33,35,60,23,40,11,27,61,3,5,7,42,45,12,59,0,55,1,44,41,14,15,..., dimensions={0} | all-to-all | bytes 1310720 | tf_op jit(solution)/shard_map/all_to_all | solution.py:293
  42.0 1.0 %merge.1 = f32[4,128]{1,0:T(4,128)S(1)} custom-call(bf16[64,40,128]{2,1,0:T(8,128)(2,1)S(1)} %all_to_all.11.got_ref, bf16[1024,128]{1,0:T(8,128)(2,1)S(1)} %get-tuple-element.26.output_ref), custom_call_target="tpu_custom_call" | custom-call | tf_op jit(solution)/shard_map/merge/pallas_call | solution.py:294
  43.0 3.6 %collective-permute-start.3 = (f32[4,128]{1,0:T(4,128)S(1)}, f32[4,128]{1,0:T(4,128)S(1)}, u32[]{:S(2)}, u32[]{:S(2)}) collective-permute-start(f32[4,128]{1,0:T(4,128)S(1)} %merge.1), channel_id=1, source_target_pairs={{0,64},{64,0},{1,65},{65,1},{2,66},{66,2},{3,67},{67,3},{4,68},{68... | collective-permute-start | bytes 6152 | tf_op jit(solution)/shard_map/ppermute | solution.py:302
  46.6 0.8 %collective-permute-done.3 = f32[4,128]{1,0:T(4,128)S(1)} collective-permute-done((f32[4,128]{1,0:T(4,128)S(1)}, f32[4,128]{1,0:T(4,128)S(1)}, u32[]{:S(2)}, u32[]{:S(2)}) %collective-permute-start.3) | collective-permute-done | bytes 2080 | tf_op jit(solution)/shard_map/ppermute | solution.py:302
  47.4 0.6 %add_convert_fusion = bf16[4,128]{1,0:T(4,128)(2,1)} fusion(f32[4,128]{1,0:T(4,128)S(1)} %merge.1, f32[4,128]{1,0:T(4,128)S(1)} %collective-permute-done.3), kind=kLoop, calls=%fused_computation | loop fusion | flops 1024 | bytes 5120 | tf_op jit(solution)/shard_map/convert_element_type | solution.py:303
  (2 shorter events, 0.0 us)
Async XLA Ops:
  17.1 8.2 %collective-permute-start.2 = (f32[40,128]{1,0:T(8,128)S(1)}, f32[40,128]{1,0:T(8,128)S(1)}, u32[]{:S(2)}, u32[]{:S(2)}) collective-permute-start(f32[40,128]{1,0:T(8,128)S(1)} %reduce_sum.9.part_ref), channel_id=1, source_target_pairs={{0,32},{32,0},{16,48},{48,16},{1,33},{33,1},{17,49},{49,17},{2,34}... | collective-permute-start | bytes 61448 | tf_op jit(solution)/shard_map/ppermute | solution.py:28
  20.8 4.5 %collective-permute-start.1 = (f32[40,128]{1,0:T(8,128)S(1)}, f32[40,128]{1,0:T(8,128)S(1)}, u32[]{:S(2)}, u32[]{:S(2)}) collective-permute-start(f32[40,128]{1,0:T(8,128)S(1)} %reduce_sum.9.part_ref), channel_id=1, source_target_pairs={{0,48},{16,0},{32,16},{48,32},{1,49},{17,1},{33,17},{49,33},{2,50}... | collective-permute-start | bytes 61448 | tf_op jit(solution)/shard_map/ppermute | solution.py:27
  21.2 4.1 %collective-permute-start = (f32[40,128]{1,0:T(8,128)S(1)}, f32[40,128]{1,0:T(8,128)S(1)}, u32[]{:S(2)}, u32[]{:S(2)}) collective-permute-start(f32[40,128]{1,0:T(8,128)S(1)} %reduce_sum.9.part_ref), channel_id=1, source_target_pairs={{0,16},{16,32},{32,48},{48,0},{1,17},{17,33},{33,49},{49,1},{2,18}... | collective-permute-start | bytes 61448 | tf_op jit(solution)/shard_map/ppermute | solution.py:26
  43.0 4.5 %collective-permute-start.3 = (f32[4,128]{1,0:T(4,128)S(1)}, f32[4,128]{1,0:T(4,128)S(1)}, u32[]{:S(2)}, u32[]{:S(2)}) collective-permute-start(f32[4,128]{1,0:T(4,128)S(1)} %merge.1), channel_id=1, source_target_pairs={{0,64},{64,0},{1,65},{65,1},{2,66},{66,2},{3,67},{67,3},{4,68},{68... | collective-permute-start | bytes 6152 | tf_op jit(solution)/shard_map/ppermute | solution.py:302

commit v7 on v6

--- a/solution.py
+++ b/solution.py
@@ -17,6 +17,7 @@
     36, 51, 21, 4, 43, 52, 9, 38, 34, 58, 39, 6, 46, 18, 8, 57,
     13, 37, 22, 30, 19, 53, 50, 25, 31, 32, 16, 2, 26, 56, 48, 49,
 )
+MIXED_PLANE = (10, 8, 12, 1, 2, 5, 9, 15, 0, 13, 3, 6, 4, 14, 7, 11)
 
 
 rope_theta = 500000.0
@@ -256,7 +257,9 @@
         compiler_params=pltpu.CompilerParams(vmem_limit_bytes=8 << 20),
         name="project",
     )(index, left(token_input_state), left(query_matrix), left(key_value_weight))
-    got = lax.all_to_all(copies, SEQ[1:], 0, 0, tiled=True)
+    planes = range(0, lax.axis_size(SEQ), len(MIXED_PLANE))
+    groups = [[plane + chip for chip in MIXED_PLANE] for plane in planes]
+    got = lax.all_to_all(copies, SEQ, 0, 0, tiled=True, axis_index_groups=groups)
     got, later_index, rates = lax.optimization_barrier((got, index, rates))
     parts = got.sum(0)
     beside, around, across = exchanges(parts, SEQ[0])

time: 48.2 us -> 46.6 us (0.967)
  blocking collectives: 31.4 us -> 29.6 us
    all_to_all x1, blocking collectives: 15.9 us -> 13.1 us  [local(): lax.all_to_all(copies, SEQ, 0, 0, tiled=True, axis_index_groups=groups)]
    all_to_all x1, blocking collectives: 15.6 us -> 16.5 us  [local(): lax.all_to_all(message, SEQ, 0, 0, tiled=True, axis_index_groups=[list(MI...]
where the time goes in v7:
time: 46.6 us; the launch traced here: 46.3 us
  blocking collectives  29.6 us (64%)
  starting transfers between devices  8.96 us (19%)
  Pallas kernels  6.21 us (13%)
  waiting for transfers between devices  0.83 us (2%)
  other arithmetic  0.67 us (1%)
    all_to_all x1, blocking collectives, local(): lax.all_to_all(message, SEQ, 0, 0, tiled=True, axis_index_groups=[list(MI...  16.5 us
    all_to_all x1, blocking collectives, local(): lax.all_to_all(copies, SEQ, 0, 0, tiled=True, axis_index_groups=groups)  13.1 us
    ppermute x1, starting transfers between devices, local(): other = lax.ppermute(partial_value, 'kv', ((0, 1), (1, 0)))  3.81 us
    ppermute x1, starting transfers between devices, exchanges(): across = lax.ppermute(array, axis, ((0, 2), (2, 0), (1, 3), (3, 1)))  3.68 us
    pallas_call x1, Pallas kernels, local(): pl.pallas_call(prepare_kernel, out_shape=[*(pltpu.VMEM(a.shape, a.dtype)...  3 us
    pallas_call x1, Pallas kernels, local(): pl.pallas_call(project_kernel, out_shape=pltpu.VMEM((lax.axis_size(SEQ[1:...  1.15 us
    pallas_call x1, Pallas kernels, local(): pl.pallas_call(attend_kernel, out_shape=pltpu.VMEM((lax.axis_size(SEQ), c...  1.07 us
    ppermute x1, starting transfers between devices, exchanges(): beside = lax.ppermute(array, axis, ((0, 1), (1, 2), (2, 3), (3, 0)))  1.03 us
  transfers between devices with their start and end apart: 4, of which 1 were waited for; matrix products, arithmetic and copies ran while one was open for 0% of the time, Pallas kernels for 6%

profile of v7, /device:TPU:1, one launch (start us, length us, event | category | flops | bytes accessed | tf_op | source)
XLA Modules:
  0.0 46.3 jit_solution(15946342125880089224)
XLA Ops:
  0.0 0.1 maximum_bitcast_fusion.rate_ref
  0.1 1.2 %project.1 = f32[16,40,128]{2,1,0:T(8,128)S(1)} custom-call(s32[1]{0:T(128)} %bitcast.shard_ref, bf16[4,8192]{1,0:T(4,128)(2,1)} %state_ref.1, bf16[128,1024]{1,0:T(8,128)(2,1)} %query_ref.1, bf16[128,256]{1,0:T(8,128)(2,1)} %keyval_ref.1), custom_call_target="tpu_custom_call" | custom-call | tf_op jit(solution)/shard_map/project/pallas_call | solution.py:246
  1.3 13.1 %all_to_all.10 = f32[16,40,128]{2,1,0:T(8,128)S(1)} all-to-all(f32[16,40,128]{2,1,0:T(8,128)S(1)} %project.1), channel_id=1, replica_groups={{10,8,12,1,2,5,9,15,0,13,3,6,4,14,7,11},{26,24,28,17,18,21,25,31,16,29,..., dimensions={0} | all-to-all | bytes 655360 | tf_op jit(solution)/shard_map/all_to_all | solution.py:262
  14.4 3.7 %collective-permute-start.2 = (f32[40,128]{1,0:T(8,128)S(1)}, f32[40,128]{1,0:T(8,128)S(1)}, u32[]{:S(2)}, u32[]{:S(2)}) collective-permute-start(f32[40,128]{1,0:T(8,128)S(1)} %reduce_sum.9.part_ref), channel_id=1, source_target_pairs={{0,32},{32,0},{16,48},{48,16},{1,33},{33,1},{17,49},{49,17},{2,34}... | collective-permute-start | bytes 61448 | tf_op jit(solution)/shard_map/ppermute | solution.py:29
  18.1 0.4 collective-permute-start.1
  18.5 1.0 %collective-permute-start = (f32[40,128]{1,0:T(8,128)S(1)}, f32[40,128]{1,0:T(8,128)S(1)}, u32[]{:S(2)}, u32[]{:S(2)}) collective-permute-start(f32[40,128]{1,0:T(8,128)S(1)} %reduce_sum.9.part_ref), channel_id=1, source_target_pairs={{0,16},{16,32},{32,48},{48,0},{1,17},{17,33},{33,49},{49,1},{2,18}... | collective-permute-start | bytes 61448 | tf_op jit(solution)/shard_map/ppermute | solution.py:27
  19.5 3.0 %prepare.1 = (bf16[4,1,2048,128]{3,2,1,0:T(8,128)(2,1)S(1)}, bf16[4,1,2048,128]{3,2,1,0:T(8,128)(2,1)S(1)}, bf16[1024,128]{1,0:T(8,128)(2,1)S(1)}, f32[8,128]{1,...) custom-call(s32[1]{0:T(128)} %bitcast.shard_ref, s32[4,64]{1,0:T(4,128)} %live_ref.1, s32[4]{0:T(128)} %owner_ref.1, ...), custom_call_target="tpu_custom_call" | custom-call | tf_op jit(solution)/shard_map/prepare/pallas_call | solution.py:269
  22.5 0.0 collective-permute-done.2.across_ref
  22.6 0.0 collective-permute-done.1.around_ref
  22.6 0.0 collective-permute-done.beside_ref
  22.6 1.1 %attend.1 = bf16[64,40,128]{2,1,0:T(8,128)(2,1)S(1)} custom-call(f32[40,128]{1,0:T(8,128)S(1)} %reduce_sum.9.part_ref, f32[40,128]{1,0:T(8,128)S(1)} %collective-permute-done.beside_ref, f32[40,128]{1,0:T(8,128)S(1)} %collective-permute-done.1.around_ref, f32[40,128]{1,0:T(8,128)S(1)} %collective-permute-done.2.across_ref, ...), custom_call_target="tpu_custom_call" | custom-call | tf_op jit(solution)/shard_map/attend/pallas_call | solution.py:285
  23.7 16.5 %all_to_all.11.got_ref = bf16[64,40,128]{2,1,0:T(8,128)(2,1)S(1)} all-to-all(bf16[64,40,128]{2,1,0:T(8,128)(2,1)S(1)} %attend.1), channel_id=1, replica_groups={{29,28,24,33,35,60,23,40,11,27,61,3,5,7,42,45,12,59,0,55,1,44,41,14,15,..., dimensions={0} | all-to-all | bytes 1310720 | tf_op jit(solution)/shard_map/all_to_all | solution.py:296
  40.2 1.0 %merge.1 = f32[4,128]{1,0:T(4,128)S(1)} custom-call(bf16[64,40,128]{2,1,0:T(8,128)(2,1)S(1)} %all_to_all.11.got_ref, bf16[1024,128]{1,0:T(8,128)(2,1)S(1)} %get-tuple-element.26.output_ref), custom_call_target="tpu_custom_call" | custom-call | tf_op jit(solution)/shard_map/merge/pallas_call | solution.py:297
  41.1 3.8 %collective-permute-start.3 = (f32[4,128]{1,0:T(4,128)S(1)}, f32[4,128]{1,0:T(4,128)S(1)}, u32[]{:S(2)}, u32[]{:S(2)}) collective-permute-start(f32[4,128]{1,0:T(4,128)S(1)} %merge.1), channel_id=1, source_target_pairs={{0,64},{64,0},{1,65},{65,1},{2,66},{66,2},{3,67},{67,3},{4,68},{68... | collective-permute-start | bytes 6152 | tf_op jit(solution)/shard_map/ppermute | solution.py:305
  45.0 0.8 %collective-permute-done.3 = f32[4,128]{1,0:T(4,128)S(1)} collective-permute-done((f32[4,128]{1,0:T(4,128)S(1)}, f32[4,128]{1,0:T(4,128)S(1)}, u32[]{:S(2)}, u32[]{:S(2)}) %collective-permute-start.3) | collective-permute-done | bytes 2080 | tf_op jit(solution)/shard_map/ppermute | solution.py:305
  45.8 0.6 %add_convert_fusion = bf16[4,128]{1,0:T(4,128)(2,1)} fusion(f32[4,128]{1,0:T(4,128)S(1)} %merge.1, f32[4,128]{1,0:T(4,128)S(1)} %collective-permute-done.3), kind=kLoop, calls=%fused_computation | loop fusion | flops 1024 | bytes 5120 | tf_op jit(solution)/shard_map/convert_element_type | solution.py:306
  (2 shorter events, 0.0 us)
Async XLA Ops:
  14.4 8.2 %collective-permute-start.2 = (f32[40,128]{1,0:T(8,128)S(1)}, f32[40,128]{1,0:T(8,128)S(1)}, u32[]{:S(2)}, u32[]{:S(2)}) collective-permute-start(f32[40,128]{1,0:T(8,128)S(1)} %reduce_sum.9.part_ref), channel_id=1, source_target_pairs={{0,32},{32,0},{16,48},{48,16},{1,33},{33,1},{17,49},{49,17},{2,34}... | collective-permute-start | bytes 61448 | tf_op jit(solution)/shard_map/ppermute | solution.py:29
  18.1 4.5 %collective-permute-start.1 = (f32[40,128]{1,0:T(8,128)S(1)}, f32[40,128]{1,0:T(8,128)S(1)}, u32[]{:S(2)}, u32[]{:S(2)}) collective-permute-start(f32[40,128]{1,0:T(8,128)S(1)} %reduce_sum.9.part_ref), channel_id=1, source_target_pairs={{0,48},{16,0},{32,16},{48,32},{1,49},{17,1},{33,17},{49,33},{2,50}... | collective-permute-start | bytes 61448 | tf_op jit(solution)/shard_map/ppermute | solution.py:28
  18.5 4.1 %collective-permute-start = (f32[40,128]{1,0:T(8,128)S(1)}, f32[40,128]{1,0:T(8,128)S(1)}, u32[]{:S(2)}, u32[]{:S(2)}) collective-permute-start(f32[40,128]{1,0:T(8,128)S(1)} %reduce_sum.9.part_ref), channel_id=1, source_target_pairs={{0,16},{16,32},{32,48},{48,0},{1,17},{17,33},{33,49},{49,1},{2,18}... | collective-permute-start | bytes 61448 | tf_op jit(solution)/shard_map/ppermute | solution.py:27
  41.1 4.6 %collective-permute-start.3 = (f32[4,128]{1,0:T(4,128)S(1)}, f32[4,128]{1,0:T(4,128)S(1)}, u32[]{:S(2)}, u32[]{:S(2)}) collective-permute-start(f32[4,128]{1,0:T(4,128)S(1)} %merge.1), channel_id=1, source_target_pairs={{0,64},{64,0},{1,65},{65,1},{2,66},{66,2},{3,67},{67,3},{4,68},{68... | collective-permute-start | bytes 6152 | tf_op jit(solution)/shard_map/ppermute | solution.py:305

commit v8 on v5

--- a/solution.py
+++ b/solution.py
@@ -11,6 +11,8 @@
 HEAD_SIZE = 128
 QUERY_GROUP = 8
 SEQ = ("seq_0", "seq_1", "seq_2")
+MIXED_PLANE = (10, 8, 12, 1, 2, 5, 9, 15, 0, 13, 3, 6, 4, 14, 7, 11)
+MIXED = [(at + turn) % 4 * 16 + chip for at, chip in enumerate(MIXED_PLANE) for turn in range(4)]
 
 
 rope_theta = 500000.0
@@ -250,7 +252,9 @@
         compiler_params=pltpu.CompilerParams(vmem_limit_bytes=8 << 20),
         name="project",
     )(index, left(token_input_state), left(query_matrix), left(key_value_weight))
-    got = lax.all_to_all(copies, SEQ[1:], 0, 0, tiled=True)
+    planes = range(0, lax.axis_size(SEQ), len(MIXED_PLANE))
+    groups = [[plane + chip for chip in MIXED_PLANE] for plane in planes]
+    got = lax.all_to_all(copies, SEQ, 0, 0, tiled=True, axis_index_groups=groups)
     got, later_index, rates = lax.optimization_barrier((got, index, rates))
     parts = got.sum(0)
     beside, around, across = exchanges(parts, SEQ[0])
@@ -284,7 +288,7 @@
     )(
         *(held(a) for a in (parts, beside, around, across, cosine, sine, own, keys, values)),
     )
-    got = lax.all_to_all(message, SEQ, 0, 0, tiled=True)
+    got = lax.all_to_all(message, SEQ, 0, 0, tiled=True, axis_index_groups=[MIXED])
     partial_value = pl.pallas_call(
         merge_kernel,
         out_shape=pltpu.VMEM((batch_rows, HEAD_SIZE), jnp.float32),

time: 49.6 us -> 45.8 us (0.923)
  blocking collectives: 32.4 us -> 28.7 us
    all_to_all x2, blocking collectives: 32.4 us -> 28.7 us  [the longest x1 15.6 us: local(): lax.all_to_all(message, SEQ, 0, 0, tiled=True, axis_index_groups=[MIXED])]
  transfers between devices with their start and end apart: 4 -> 4, of which waited for: 1 -> 1; matrix products, arithmetic and copies ran while one was open for 0% -> 0% of each run, Pallas kernels for 6% -> 7%
where the time goes in v8:
time: 45.8 us; the launch traced here: 45.5 us
  blocking collectives  28.7 us (63%)
  starting transfers between devices  9.08 us (20%)
  Pallas kernels  6.21 us (14%)
  waiting for transfers between devices  0.83 us (2%)
  other arithmetic  0.67 us (1%)
    all_to_all x1, blocking collectives, local(): lax.all_to_all(message, SEQ, 0, 0, tiled=True, axis_index_groups=[MIXED])  15.6 us
    all_to_all x1, blocking collectives, local(): lax.all_to_all(copies, SEQ, 0, 0, tiled=True, axis_index_groups=groups)  13.1 us
    ppermute x1, starting transfers between devices, local(): other = lax.ppermute(partial_value, 'kv', ((0, 1), (1, 0)))  3.93 us
    ppermute x1, starting transfers between devices, exchanges(): across = lax.ppermute(array, axis, ((0, 2), (2, 0), (1, 3), (3, 1)))  3.68 us
    pallas_call x1, Pallas kernels, local(): pl.pallas_call(prepare_kernel, out_shape=[*(pltpu.VMEM(a.shape, a.dtype)...  3 us
    pallas_call x1, Pallas kernels, local(): pl.pallas_call(project_kernel, out_shape=pltpu.VMEM((lax.axis_size(SEQ[1:...  1.15 us
    pallas_call x1, Pallas kernels, local(): pl.pallas_call(attend_kernel, out_shape=pltpu.VMEM((lax.axis_size(SEQ), c...  1.07 us
    ppermute x1, starting transfers between devices, exchanges(): beside = lax.ppermute(array, axis, ((0, 1), (1, 2), (2, 3), (3, 0)))  1.03 us
  transfers between devices with their start and end apart: 4, of which 1 were waited for; matrix products, arithmetic and copies ran while one was open for 0% of the time, Pallas kernels for 7%

profile of v8, /device:TPU:1, one launch (start us, length us, event | category | flops | bytes accessed | tf_op | source)
XLA Modules:
  0.0 45.5 jit_solution(7637592386934232552)
XLA Ops:
  0.0 0.1 maximum_bitcast_fusion.rate_ref
  0.1 1.2 %project.1 = f32[16,40,128]{2,1,0:T(8,128)S(1)} custom-call(s32[1]{0:T(128)} %bitcast.shard_ref, bf16[4,8192]{1,0:T(4,128)(2,1)} %state_ref.1, bf16[128,1024]{1,0:T(8,128)(2,1)} %query_ref.1, bf16[128,256]{1,0:T(8,128)(2,1)} %keyval_ref.1), custom_call_target="tpu_custom_call" | custom-call | tf_op jit(solution)/shard_map/project/pallas_call | solution.py:241
  1.3 13.1 %all_to_all.10 = f32[16,40,128]{2,1,0:T(8,128)S(1)} all-to-all(f32[16,40,128]{2,1,0:T(8,128)S(1)} %project.1), channel_id=1, replica_groups={{10,8,12,1,2,5,9,15,0,13,3,6,4,14,7,11},{26,24,28,17,18,21,25,31,16,29,..., dimensions={0} | all-to-all | bytes 655360 | tf_op jit(solution)/shard_map/all_to_all | solution.py:257
  14.4 3.7 %collective-permute-start.2 = (f32[40,128]{1,0:T(8,128)S(1)}, f32[40,128]{1,0:T(8,128)S(1)}, u32[]{:S(2)}, u32[]{:S(2)}) collective-permute-start(f32[40,128]{1,0:T(8,128)S(1)} %reduce_sum.9.part_ref), channel_id=1, source_target_pairs={{0,32},{32,0},{16,48},{48,16},{1,33},{33,1},{17,49},{49,17},{2,34}... | collective-permute-start | bytes 61448 | tf_op jit(solution)/shard_map/ppermute | solution.py:24
  18.1 0.4 collective-permute-start.1
  18.5 1.0 %collective-permute-start = (f32[40,128]{1,0:T(8,128)S(1)}, f32[40,128]{1,0:T(8,128)S(1)}, u32[]{:S(2)}, u32[]{:S(2)}) collective-permute-start(f32[40,128]{1,0:T(8,128)S(1)} %reduce_sum.9.part_ref), channel_id=1, source_target_pairs={{0,16},{16,32},{32,48},{48,0},{1,17},{17,33},{33,49},{49,1},{2,18}... | collective-permute-start | bytes 61448 | tf_op jit(solution)/shard_map/ppermute | solution.py:22
  19.5 3.0 %prepare.1 = (bf16[4,1,2048,128]{3,2,1,0:T(8,128)(2,1)S(1)}, bf16[4,1,2048,128]{3,2,1,0:T(8,128)(2,1)S(1)}, bf16[1024,128]{1,0:T(8,128)(2,1)S(1)}, f32[8,128]{1,...) custom-call(s32[1]{0:T(128)} %bitcast.shard_ref, s32[4,64]{1,0:T(4,128)} %live_ref.1, s32[4]{0:T(128)} %owner_ref.1, ...), custom_call_target="tpu_custom_call" | custom-call | tf_op jit(solution)/shard_map/prepare/pallas_call | solution.py:264
  22.5 0.0 collective-permute-done.2.across_ref
  22.6 0.0 collective-permute-done.1.around_ref
  22.6 0.0 collective-permute-done.beside_ref
  22.6 1.1 %attend.1 = bf16[64,40,128]{2,1,0:T(8,128)(2,1)S(1)} custom-call(f32[40,128]{1,0:T(8,128)S(1)} %reduce_sum.9.part_ref, f32[40,128]{1,0:T(8,128)S(1)} %collective-permute-done.beside_ref, f32[40,128]{1,0:T(8,128)S(1)} %collective-permute-done.1.around_ref, f32[40,128]{1,0:T(8,128)S(1)} %collective-permute-done.2.across_ref, ...), custom_call_target="tpu_custom_call" | custom-call | tf_op jit(solution)/shard_map/attend/pallas_call | solution.py:280
  23.7 15.6 %all_to_all.11.got_ref = bf16[64,40,128]{2,1,0:T(8,128)(2,1)S(1)} all-to-all(bf16[64,40,128]{2,1,0:T(8,128)(2,1)S(1)} %attend.1), channel_id=1, replica_groups={{10,26,42,58,24,40,56,8,44,60,12,28,49,1,17,33,2,18,34,50,21,37,53,5,41..., dimensions={0} | all-to-all | bytes 1310720 | tf_op jit(solution)/shard_map/all_to_all | solution.py:291
  39.2 1.0 %merge.1 = f32[4,128]{1,0:T(4,128)S(1)} custom-call(bf16[64,40,128]{2,1,0:T(8,128)(2,1)S(1)} %all_to_all.11.got_ref, bf16[1024,128]{1,0:T(8,128)(2,1)S(1)} %get-tuple-element.26.output_ref), custom_call_target="tpu_custom_call" | custom-call | tf_op jit(solution)/shard_map/merge/pallas_call | solution.py:292
  40.2 3.9 %collective-permute-start.3 = (f32[4,128]{1,0:T(4,128)S(1)}, f32[4,128]{1,0:T(4,128)S(1)}, u32[]{:S(2)}, u32[]{:S(2)}) collective-permute-start(f32[4,128]{1,0:T(4,128)S(1)} %merge.1), channel_id=1, source_target_pairs={{0,64},{64,0},{1,65},{65,1},{2,66},{66,2},{3,67},{67,3},{4,68},{68... | collective-permute-start | bytes 6152 | tf_op jit(solution)/shard_map/ppermute | solution.py:300
  44.2 0.8 %collective-permute-done.3 = f32[4,128]{1,0:T(4,128)S(1)} collective-permute-done((f32[4,128]{1,0:T(4,128)S(1)}, f32[4,128]{1,0:T(4,128)S(1)}, u32[]{:S(2)}, u32[]{:S(2)}) %collective-permute-start.3) | collective-permute-done | bytes 2080 | tf_op jit(solution)/shard_map/ppermute | solution.py:300
  45.0 0.6 %add_convert_fusion = bf16[4,128]{1,0:T(4,128)(2,1)} fusion(f32[4,128]{1,0:T(4,128)S(1)} %merge.1, f32[4,128]{1,0:T(4,128)S(1)} %collective-permute-done.3), kind=kLoop, calls=%fused_computation | loop fusion | flops 1024 | bytes 5120 | tf_op jit(solution)/shard_map/convert_element_type | solution.py:301
  (2 shorter events, 0.0 us)
Async XLA Ops:
  14.4 8.2 %collective-permute-start.2 = (f32[40,128]{1,0:T(8,128)S(1)}, f32[40,128]{1,0:T(8,128)S(1)}, u32[]{:S(2)}, u32[]{:S(2)}) collective-permute-start(f32[40,128]{1,0:T(8,128)S(1)} %reduce_sum.9.part_ref), channel_id=1, source_target_pairs={{0,32},{32,0},{16,48},{48,16},{1,33},{33,1},{17,49},{49,17},{2,34}... | collective-permute-start | bytes 61448 | tf_op jit(solution)/shard_map/ppermute | solution.py:24
  18.1 4.5 %collective-permute-start.1 = (f32[40,128]{1,0:T(8,128)S(1)}, f32[40,128]{1,0:T(8,128)S(1)}, u32[]{:S(2)}, u32[]{:S(2)}) collective-permute-start(f32[40,128]{1,0:T(8,128)S(1)} %reduce_sum.9.part_ref), channel_id=1, source_target_pairs={{0,48},{16,0},{32,16},{48,32},{1,49},{17,1},{33,17},{49,33},{2,50}... | collective-permute-start | bytes 61448 | tf_op jit(solution)/shard_map/ppermute | solution.py:23
  18.5 4.1 %collective-permute-start = (f32[40,128]{1,0:T(8,128)S(1)}, f32[40,128]{1,0:T(8,128)S(1)}, u32[]{:S(2)}, u32[]{:S(2)}) collective-permute-start(f32[40,128]{1,0:T(8,128)S(1)} %reduce_sum.9.part_ref), channel_id=1, source_target_pairs={{0,16},{16,32},{32,48},{48,0},{1,17},{17,33},{33,49},{49,1},{2,18}... | collective-permute-start | bytes 61448 | tf_op jit(solution)/shard_map/ppermute | solution.py:22
  40.2 4.8 %collective-permute-start.3 = (f32[4,128]{1,0:T(4,128)S(1)}, f32[4,128]{1,0:T(4,128)S(1)}, u32[]{:S(2)}, u32[]{:S(2)}) collective-permute-start(f32[4,128]{1,0:T(4,128)S(1)} %merge.1), channel_id=1, source_target_pairs={{0,64},{64,0},{1,65},{65,1},{2,66},{66,2},{3,67},{67,3},{4,68},{68... | collective-permute-start | bytes 6152 | tf_op jit(solution)/shard_map/ppermute | solution.py:300

commit v9 on v8

--- a/solution.py
+++ b/solution.py
@@ -12,6 +12,7 @@
 QUERY_GROUP = 8
 SEQ = ("seq_0", "seq_1", "seq_2")
 MIXED_PLANE = (10, 8, 12, 1, 2, 5, 9, 15, 0, 13, 3, 6, 4, 14, 7, 11)
+FIRST_PLANE = (10, 14, 5, 1, 9, 2, 3, 11, 13, 7, 8, 4, 0, 6, 15, 12)
 MIXED = [(at + turn) % 4 * 16 + chip for at, chip in enumerate(MIXED_PLANE) for turn in range(4)]
 
 
@@ -252,8 +253,8 @@
         compiler_params=pltpu.CompilerParams(vmem_limit_bytes=8 << 20),
         name="project",
     )(index, left(token_input_state), left(query_matrix), left(key_value_weight))
-    planes = range(0, lax.axis_size(SEQ), len(MIXED_PLANE))
-    groups = [[plane + chip for chip in MIXED_PLANE] for plane in planes]
+    planes = range(0, lax.axis_size(SEQ), len(FIRST_PLANE))
+    groups = [[plane + chip for chip in FIRST_PLANE] for plane in planes]
     got = lax.all_to_all(copies, SEQ, 0, 0, tiled=True, axis_index_groups=groups)
     got, later_index, rates = lax.optimization_barrier((got, index, rates))
     parts = got.sum(0)

time: 45.8 us -> 46.3 us (1.011)
  blocking collectives: 28.7 us -> 29.2 us
    all_to_all x1, blocking collectives: 15.6 us -> 16.9 us  [local(): lax.all_to_all(message, SEQ, 0, 0, tiled=True, axis_index_groups=[MIXED])]
    all_to_all x1, blocking collectives: 13.1 us -> 12.3 us  [local(): lax.all_to_all(copies, SEQ, 0, 0, tiled=True, axis_index_groups=groups)]
where the time goes in v9:
time: 46.3 us; the launch traced here: 46.1 us
  blocking collectives  29.2 us (63%)
  starting transfers between devices  9.09 us (20%)
  Pallas kernels  6.21 us (13%)
  waiting for transfers between devices  0.83 us (2%)
  other arithmetic  0.67 us (1%)
    all_to_all x1, blocking collectives, local(): lax.all_to_all(message, SEQ, 0, 0, tiled=True, axis_index_groups=[MIXED])  16.9 us
    all_to_all x1, blocking collectives, local(): lax.all_to_all(copies, SEQ, 0, 0, tiled=True, axis_index_groups=groups)  12.3 us
    ppermute x1, starting transfers between devices, local(): other = lax.ppermute(partial_value, 'kv', ((0, 1), (1, 0)))  3.95 us
    ppermute x1, starting transfers between devices, exchanges(): across = lax.ppermute(array, axis, ((0, 2), (2, 0), (1, 3), (3, 1)))  3.68 us
    pallas_call x1, Pallas kernels, local(): pl.pallas_call(prepare_kernel, out_shape=[*(pltpu.VMEM(a.shape, a.dtype)...  3 us
    pallas_call x1, Pallas kernels, local(): pl.pallas_call(project_kernel, out_shape=pltpu.VMEM((lax.axis_size(SEQ[1:...  1.15 us
    pallas_call x1, Pallas kernels, local(): pl.pallas_call(attend_kernel, out_shape=pltpu.VMEM((lax.axis_size(SEQ), c...  1.07 us
    ppermute x1, starting transfers between devices, exchanges(): beside = lax.ppermute(array, axis, ((0, 1), (1, 2), (2, 3), (3, 0)))  1.03 us
  transfers between devices with their start and end apart: 4, of which 1 were waited for; matrix products, arithmetic and copies ran while one was open for 0% of the time, Pallas kernels for 7%

profile of v9, /device:TPU:1, one launch (start us, length us, event | category | flops | bytes accessed | tf_op | source)
XLA Modules:
  0.0 46.1 jit_solution(15346195313660334402)
XLA Ops:
  0.0 0.1 maximum_bitcast_fusion.rate_ref
  0.1 1.2 %project.1 = f32[16,40,128]{2,1,0:T(8,128)S(1)} custom-call(s32[1]{0:T(128)} %bitcast.shard_ref, bf16[4,8192]{1,0:T(4,128)(2,1)} %state_ref.1, bf16[128,1024]{1,0:T(8,128)(2,1)} %query_ref.1, bf16[128,256]{1,0:T(8,128)(2,1)} %keyval_ref.1), custom_call_target="tpu_custom_call" | custom-call | tf_op jit(solution)/shard_map/project/pallas_call | solution.py:242
  1.3 12.3 %all_to_all.10 = f32[16,40,128]{2,1,0:T(8,128)S(1)} all-to-all(f32[16,40,128]{2,1,0:T(8,128)S(1)} %project.1), channel_id=1, replica_groups={{10,14,5,1,9,2,3,11,13,7,8,4,0,6,15,12},{26,30,21,17,25,18,19,27,29,23,..., dimensions={0} | all-to-all | bytes 655360 | tf_op jit(solution)/shard_map/all_to_all | solution.py:258
  13.6 3.7 %collective-permute-start.2 = (f32[40,128]{1,0:T(8,128)S(1)}, f32[40,128]{1,0:T(8,128)S(1)}, u32[]{:S(2)}, u32[]{:S(2)}) collective-permute-start(f32[40,128]{1,0:T(8,128)S(1)} %reduce_sum.9.part_ref), channel_id=1, source_target_pairs={{0,32},{32,0},{16,48},{48,16},{1,33},{33,1},{17,49},{49,17},{2,34}... | collective-permute-start | bytes 61448 | tf_op jit(solution)/shard_map/ppermute | solution.py:25
  17.3 0.4 collective-permute-start.1
  17.7 1.0 %collective-permute-start = (f32[40,128]{1,0:T(8,128)S(1)}, f32[40,128]{1,0:T(8,128)S(1)}, u32[]{:S(2)}, u32[]{:S(2)}) collective-permute-start(f32[40,128]{1,0:T(8,128)S(1)} %reduce_sum.9.part_ref), channel_id=1, source_target_pairs={{0,16},{16,32},{32,48},{48,0},{1,17},{17,33},{33,49},{49,1},{2,18}... | collective-permute-start | bytes 61448 | tf_op jit(solution)/shard_map/ppermute | solution.py:23
  18.7 3.0 %prepare.1 = (bf16[4,1,2048,128]{3,2,1,0:T(8,128)(2,1)S(1)}, bf16[4,1,2048,128]{3,2,1,0:T(8,128)(2,1)S(1)}, bf16[1024,128]{1,0:T(8,128)(2,1)S(1)}, f32[8,128]{1,...) custom-call(s32[1]{0:T(128)} %bitcast.shard_ref, s32[4,64]{1,0:T(4,128)} %live_ref.1, s32[4]{0:T(128)} %owner_ref.1, ...), custom_call_target="tpu_custom_call" | custom-call | tf_op jit(solution)/shard_map/prepare/pallas_call | solution.py:265
  21.7 0.0 collective-permute-done.2.across_ref
  21.7 0.0 collective-permute-done.1.around_ref
  21.8 0.0 collective-permute-done.beside_ref
  21.8 1.1 %attend.1 = bf16[64,40,128]{2,1,0:T(8,128)(2,1)S(1)} custom-call(f32[40,128]{1,0:T(8,128)S(1)} %reduce_sum.9.part_ref, f32[40,128]{1,0:T(8,128)S(1)} %collective-permute-done.beside_ref, f32[40,128]{1,0:T(8,128)S(1)} %collective-permute-done.1.around_ref, f32[40,128]{1,0:T(8,128)S(1)} %collective-permute-done.2.across_ref, ...), custom_call_target="tpu_custom_call" | custom-call | tf_op jit(solution)/shard_map/attend/pallas_call | solution.py:281
  22.8 16.9 %all_to_all.11.got_ref = bf16[64,40,128]{2,1,0:T(8,128)(2,1)S(1)} all-to-all(bf16[64,40,128]{2,1,0:T(8,128)(2,1)S(1)} %attend.1), channel_id=1, replica_groups={{10,26,42,58,24,40,56,8,44,60,12,28,49,1,17,33,2,18,34,50,21,37,53,5,41..., dimensions={0} | all-to-all | bytes 1310720 | tf_op jit(solution)/shard_map/all_to_all | solution.py:292
  39.8 1.0 %merge.1 = f32[4,128]{1,0:T(4,128)S(1)} custom-call(bf16[64,40,128]{2,1,0:T(8,128)(2,1)S(1)} %all_to_all.11.got_ref, bf16[1024,128]{1,0:T(8,128)(2,1)S(1)} %get-tuple-element.26.output_ref), custom_call_target="tpu_custom_call" | custom-call | tf_op jit(solution)/shard_map/merge/pallas_call | solution.py:293
  40.8 3.9 %collective-permute-start.3 = (f32[4,128]{1,0:T(4,128)S(1)}, f32[4,128]{1,0:T(4,128)S(1)}, u32[]{:S(2)}, u32[]{:S(2)}) collective-permute-start(f32[4,128]{1,0:T(4,128)S(1)} %merge.1), channel_id=1, source_target_pairs={{0,64},{64,0},{1,65},{65,1},{2,66},{66,2},{3,67},{67,3},{4,68},{68... | collective-permute-start | bytes 6152 | tf_op jit(solution)/shard_map/ppermute | solution.py:301
  44.7 0.8 %collective-permute-done.3 = f32[4,128]{1,0:T(4,128)S(1)} collective-permute-done((f32[4,128]{1,0:T(4,128)S(1)}, f32[4,128]{1,0:T(4,128)S(1)}, u32[]{:S(2)}, u32[]{:S(2)}) %collective-permute-start.3) | collective-permute-done | bytes 2080 | tf_op jit(solution)/shard_map/ppermute | solution.py:301
  45.5 0.6 %add_convert_fusion = bf16[4,128]{1,0:T(4,128)(2,1)} fusion(f32[4,128]{1,0:T(4,128)S(1)} %merge.1, f32[4,128]{1,0:T(4,128)S(1)} %collective-permute-done.3), kind=kLoop, calls=%fused_computation | loop fusion | flops 1024 | bytes 5120 | tf_op jit(solution)/shard_map/convert_element_type | solution.py:302
  (2 shorter events, 0.0 us)
Async XLA Ops:
  13.6 8.2 %collective-permute-start.2 = (f32[40,128]{1,0:T(8,128)S(1)}, f32[40,128]{1,0:T(8,128)S(1)}, u32[]{:S(2)}, u32[]{:S(2)}) collective-permute-start(f32[40,128]{1,0:T(8,128)S(1)} %reduce_sum.9.part_ref), channel_id=1, source_target_pairs={{0,32},{32,0},{16,48},{48,16},{1,33},{33,1},{17,49},{49,17},{2,34}... | collective-permute-start | bytes 61448 | tf_op jit(solution)/shard_map/ppermute | solution.py:25
  17.3 4.5 %collective-permute-start.1 = (f32[40,128]{1,0:T(8,128)S(1)}, f32[40,128]{1,0:T(8,128)S(1)}, u32[]{:S(2)}, u32[]{:S(2)}) collective-permute-start(f32[40,128]{1,0:T(8,128)S(1)} %reduce_sum.9.part_ref), channel_id=1, source_target_pairs={{0,48},{16,0},{32,16},{48,32},{1,49},{17,1},{33,17},{49,33},{2,50}... | collective-permute-start | bytes 61448 | tf_op jit(solution)/shard_map/ppermute | solution.py:24
  17.7 4.1 %collective-permute-start = (f32[40,128]{1,0:T(8,128)S(1)}, f32[40,128]{1,0:T(8,128)S(1)}, u32[]{:S(2)}, u32[]{:S(2)}) collective-permute-start(f32[40,128]{1,0:T(8,128)S(1)} %reduce_sum.9.part_ref), channel_id=1, source_target_pairs={{0,16},{16,32},{32,48},{48,0},{1,17},{17,33},{33,49},{49,1},{2,18}... | collective-permute-start | bytes 61448 | tf_op jit(solution)/shard_map/ppermute | solution.py:23
  40.8 4.8 %collective-permute-start.3 = (f32[4,128]{1,0:T(4,128)S(1)}, f32[4,128]{1,0:T(4,128)S(1)}, u32[]{:S(2)}, u32[]{:S(2)}) collective-permute-start(f32[4,128]{1,0:T(4,128)S(1)} %merge.1), channel_id=1, source_target_pairs={{0,64},{64,0},{1,65},{65,1},{2,66},{66,2},{3,67},{67,3},{4,68},{68... | collective-permute-start | bytes 6152 | tf_op jit(solution)/shard_map/ppermute | solution.py:301
